TPU v7x, 32 devices: a whole 2x2x4 slice. The times are simulated.
32 devices in a mesh: batch: 8 (over z, y), seq: 4 (over x, core).
Axes of the slice: x: 2, y: 2, z: 4, core: 2. Of those that a mesh axis runs over, the one named last changes fastest.
Arguments:
- tokens: bfloat16 [24, 1024, 1024], P('batch', 'seq'), may hold values from -6 to 6
- lengths: int32 [16], replicated, may hold values from 150 to 1024, as said below
- assignment: int32 [24], P('batch'), may hold values from -1 to 15, as said below
- query_weight: bfloat16 [1024, 1024], P(None, 'seq'), may hold values from -0.1875 to 0.1875
- key_weight: bfloat16 [1024, 1024], P(None, 'seq'), may hold values from -0.1875 to 0.1875
- value_weight: bfloat16 [1024, 1024], P(None, 'seq'), may hold values from -0.1875 to 0.1875
- gate_weight: bfloat16 [1024, 1024], P(None, 'seq'), may hold values from -0.1875 to 0.1875
- out_weight: bfloat16 [1024, 1024], P('seq'), may hold values from -0.375 to 0.375
- up_weight: bfloat16 [1024, 2816], P(None, 'seq'), may hold values from -0.1875 to 0.1875
- pair_weight: bfloat16 [1024, 2816], P(None, 'seq'), may hold values from -0.1875 to 0.1875
- down_weight: bfloat16 [2816, 1024], P('seq'), may hold values from -0.109375 to 0.109375
- attention_norm_gain: float32 [1024], replicated, may hold values from 0.5 to 1.5
- mlp_gain: float32 [1024], replicated, may hold values from 0.5 to 1.5
- head_gain: float32 [1024], P('seq'), may hold values from 0.5 to 1.5
- cotangent: bfloat16 [24, 1024, 1024], P('batch', 'seq'), may hold values from -6 to 6
Outputs:
- result: bfloat16 [24, 1024, 1024], P('batch', 'seq')
- grad_tokens: float32 [24, 1024, 1024], P('batch', 'seq')
- grad_query_weight: float32 [1024, 1024], P(None, 'seq')
- grad_key_weight: float32 [1024, 1024], P(None, 'seq')
- grad_value_weight: float32 [1024, 1024], P(None, 'seq')
- grad_gate_weight: float32 [1024, 1024], P(None, 'seq')
- grad_out_weight: float32 [1024, 1024], P('seq')
- grad_up_weight: float32 [1024, 2816], P(None, 'seq')
- grad_pair_weight: float32 [1024, 2816], P(None, 'seq')
- grad_down_weight: float32 [2816, 1024], P('seq')
- grad_attention_gain: float32 [1024], replicated
- grad_mlp_gain: float32 [1024], replicated
- grad_head_gain: float32 [1024], P('seq')
Inputs may be any that keep to these rules, and one draw needn't show every extreme that they name: `lengths`: the true tokens of each sequence; positions from the length on are padding and give no keys. `assignment`: each sequence stands in exactly one slot; the slots come in groups of 3 consecutive slots; each group holds 1 to 3 sequences in its first slots, the rest are -1.
All inputs are finite; a program needn't handle non-finite values.
Results may differ from a plain program's by a relative error of at most 0.025.
Values may be sent and summed in bfloat16 or wider, within the bound.
A program may use at most 256 MiB of HBM per device.

v0:
```python
import jax
import jax.numpy as jnp
from jax import lax
from jax.sharding import PartitionSpec as P

HD = 64


EPS = 1e-05


def normalize(values, gain):
    scale = lax.rsqrt(jnp.mean(values * values, axis=-1, keepdims=True) + EPS)
    normed = values * scale
    return (normed, scale, normed * gain)


def norm_back(grad_out, normed, scale, gain):
    grad_normed = grad_out * gain
    inner = jnp.mean(grad_normed * normed, axis=-1, keepdims=True)
    return scale * (grad_normed - normed * inner)


def matmul(left_operand, right_operand):
    return lax.dot_general(
        left_operand,
        right_operand,
        (((left_operand.ndim - 1,), (0,)), ((), ())),
        preferred_element_type=jnp.float32,
    )


def matmul_back(left_operand, right_operand):
    return lax.dot_general(
        left_operand,
        right_operand,
        (((left_operand.ndim - 1,), (1,)), ((), ())),
        preferred_element_type=jnp.float32,
    )


def weight_grad(inputs, grads):
    return lax.dot_general(
        inputs, grads, (((0, 1), (0, 1)), ((), ())), preferred_element_type=jnp.float32
    )


def causal_mask(length):
    rows = lax.broadcasted_iota(jnp.int32, (length, length), 0)
    cols = lax.broadcasted_iota(jnp.int32, (length, length), 1)
    return rows >= cols


def attend_one(parts):
    query, keys, values = parts
    keep = causal_mask(query.shape[0])
    scores = jnp.einsum("ihe,jhe->hij", query, keys, preferred_element_type=jnp.float32)
    weight_tree = jnp.where(keep[None], scores, 0.0).astype(jnp.bfloat16)
    return jnp.einsum("hij,jhe->ihe", weight_tree, values, preferred_element_type=jnp.float32)


def attend_back(parts):
    query, keys, values, grad_mixed = parts
    keep = causal_mask(query.shape[0])
    scores = jnp.einsum("ihe,jhe->hij", query, keys, preferred_element_type=jnp.float32)
    weight_tree = jnp.where(keep[None], scores, 0.0).astype(jnp.bfloat16)
    grad_scores = jnp.einsum("ihe,jhe->hij", grad_mixed, values, preferred_element_type=jnp.float32)
    grad_scores = jnp.where(keep[None], grad_scores, 0.0).astype(jnp.bfloat16)
    grad_values = jnp.einsum(
        "hij,ihe->jhe", weight_tree, grad_mixed, preferred_element_type=jnp.float32
    ).astype(jnp.bfloat16)
    grad_query = jnp.einsum(
        "hij,jhe->ihe", grad_scores, keys, preferred_element_type=jnp.float32
    ).astype(jnp.bfloat16)
    grad_keys = jnp.einsum(
        "hij,ihe->jhe", grad_scores, query, preferred_element_type=jnp.float32
    ).astype(jnp.bfloat16)
    return (grad_query, grad_keys, grad_values)


def on_device(
    tokens,
    lengths,
    assignment,
    query_weight,
    key_weight,
    value_weight,
    gate_weight,
    out_weight,
    up_weight,
    pair_weight,
    down_weight,
    attention_norm_gain,
    mlp_gain,
    head_gain,
    cotangent,
):
    local = jnp.transpose(tokens, (1, 0, 2)).astype(jnp.float32)
    normed_one, scale_one, scaled_one = normalize(local, attention_norm_gain)
    gathered_one = lax.all_gather(scaled_one.astype(jnp.bfloat16), "seq", axis=0, tiled=True)
    full_len = gathered_one.shape[0]
    slots = gathered_one.shape[1]
    width = query_weight.shape[1]
    heads_here = width // HD
    joined = jnp.concatenate([query_weight, key_weight, value_weight, gate_weight], axis=1)
    projected = matmul(gathered_one, joined)
    pre_query = projected[..., :width]
    pre_key = projected[..., width : 2 * width]
    pre_value = projected[..., 2 * width : 3 * width]
    pre_gate = projected[..., 3 * width :]
    seq_ids = lax.broadcasted_iota(jnp.int32, (slots, lengths.shape[0]), 1)
    slot_length = jnp.sum(jnp.where(assignment[:, None] == seq_ids, lengths[None, :], 0), axis=1)
    positions = lax.broadcasted_iota(jnp.int32, (full_len, slots), 0)
    valid = (positions < slot_length[None, :]).astype(jnp.float32)
    query = jax.nn.softplus(pre_query).astype(jnp.bfloat16)
    keys = (jax.nn.softplus(pre_key) * valid[..., None]).astype(jnp.bfloat16)
    values = pre_value.astype(jnp.bfloat16)

    def to_heads(array):
        return jnp.moveaxis(array.reshape(full_len, slots, heads_here, HD), 1, 0)

    def from_heads(array):
        return jnp.moveaxis(array, 0, 1).reshape(full_len, slots, width)

    query_heads, key_heads, value_heads = (to_heads(query), to_heads(keys), to_heads(values))
    mixed = jnp.moveaxis(lax.map(attend_one, (query_heads, key_heads, value_heads)), 0, 1)
    gain_heads = head_gain.reshape(heads_here, HD)
    head_normed, head_scale, head_out = normalize(mixed, gain_heads)
    head_flat = head_out.reshape(full_len, slots, width)
    gate_act = jax.nn.silu(pre_gate)
    gated = (head_flat * gate_act).astype(jnp.bfloat16)
    middle = local + lax.psum_scatter(
        matmul(gated, out_weight).astype(jnp.bfloat16), "seq", scatter_dimension=0, tiled=True
    ).astype(jnp.float32)
    normed_two, scale_two, scaled_two = normalize(middle, mlp_gain)
    gathered_two = lax.all_gather(scaled_two.astype(jnp.bfloat16), "seq", axis=0, tiled=True)
    up_part = matmul(gathered_two, up_weight)
    pair_part = matmul(gathered_two, pair_weight)
    product = (up_part * pair_part).astype(jnp.bfloat16)
    final = middle + lax.psum_scatter(
        matmul(product, down_weight).astype(jnp.bfloat16), "seq", scatter_dimension=0, tiled=True
    ).astype(jnp.float32)
    result = jnp.transpose(final, (1, 0, 2)).astype(jnp.bfloat16)
    grad_local_part = jnp.transpose(cotangent, (1, 0, 2))
    grad_full = lax.all_gather(grad_local_part, "seq", axis=0, tiled=True)
    grad_down = weight_grad(product, grad_full)
    grad_product = matmul_back(grad_full, down_weight).astype(jnp.bfloat16)
    grad_up = (grad_product * pair_part).astype(jnp.bfloat16)
    grad_pair = (grad_product * up_part).astype(jnp.bfloat16)
    grad_upw = weight_grad(gathered_two, grad_up)
    grad_pairw = weight_grad(gathered_two, grad_pair)
    grad_scaled_two = lax.psum_scatter(
        (matmul_back(grad_up, up_weight) + matmul_back(grad_pair, pair_weight)).astype(
            jnp.bfloat16
        ),
        "seq",
        scatter_dimension=0,
        tiled=True,
    ).astype(jnp.float32)
    gain_two_part = jnp.sum(grad_scaled_two * normed_two, axis=(0, 1))
    grad_middle = grad_local_part.astype(jnp.float32) + norm_back(
        grad_scaled_two, normed_two, scale_two, mlp_gain
    )
    grad_middle_full = lax.all_gather(grad_middle.astype(jnp.bfloat16), "seq", axis=0, tiled=True)
    grad_outw = weight_grad(gated, grad_middle_full)
    grad_gated = matmul_back(grad_middle_full, out_weight).astype(jnp.bfloat16)
    sigmoid_gate = jax.nn.sigmoid(pre_gate)
    grad_gate = (
        grad_gated * head_flat * sigmoid_gate * (1.0 + pre_gate * (1.0 - sigmoid_gate))
    ).astype(jnp.bfloat16)
    grad_head = (grad_gated * gate_act).reshape(full_len, slots, heads_here, HD)
    head_gain_part = jnp.sum(grad_head * head_normed, axis=(0, 1)).reshape(width)
    grad_mixed = norm_back(grad_head, head_normed, head_scale, gain_heads).astype(jnp.bfloat16)
    grad_q, grad_k, grad_v = lax.map(
        attend_back, (query_heads, key_heads, value_heads, jnp.moveaxis(grad_mixed, 1, 0))
    )
    grad_pre_query = from_heads(grad_q) * jax.nn.sigmoid(pre_query)
    grad_pre_key = from_heads(grad_k) * jax.nn.sigmoid(pre_key) * valid[..., None]
    grad_pre = jnp.concatenate(
        [
            grad_pre_query,
            grad_pre_key,
            from_heads(grad_v).astype(jnp.float32),
            grad_gate.astype(jnp.float32),
        ],
        axis=-1,
    ).astype(jnp.bfloat16)
    grad_joined = weight_grad(gathered_one, grad_pre)
    grad_scaled_one = lax.psum_scatter(
        matmul_back(grad_pre, joined).astype(jnp.bfloat16), "seq", scatter_dimension=0, tiled=True
    ).astype(jnp.float32)
    gain_one_part = jnp.sum(grad_scaled_one * normed_one, axis=(0, 1))
    grad_inputs = grad_middle + norm_back(
        grad_scaled_one, normed_one, scale_one, attention_norm_gain
    )
    gain_one, gain_two = lax.psum((gain_one_part, gain_two_part), ("batch", "seq"))
    grad_qw = grad_joined[:, :width]
    grad_kw = grad_joined[:, width : 2 * width]
    grad_vw = grad_joined[:, 2 * width : 3 * width]
    grad_gw = grad_joined[:, 3 * width :]
    (
        grad_qw,
        grad_kw,
        grad_vw,
        grad_gw,
        grad_outw,
        grad_upw,
        grad_pairw,
        grad_down,
        head_gain_total,
    ) = lax.psum(
        (
            grad_qw,
            grad_kw,
            grad_vw,
            grad_gw,
            grad_outw,
            grad_upw,
            grad_pairw,
            grad_down,
            head_gain_part,
        ),
        "batch",
    )
    return (
        result,
        jnp.transpose(grad_inputs, (1, 0, 2)),
        grad_qw,
        grad_kw,
        grad_vw,
        grad_gw,
        grad_outw,
        grad_upw,
        grad_pairw,
        grad_down,
        gain_one,
        gain_two,
        head_gain_total,
    )


def solution(mesh):
    return jax.shard_map(
        on_device,
        mesh=mesh,
        in_specs=(
            P("batch", "seq", None),
            P(),
            P("batch"),
            P(None, "seq"),
            P(None, "seq"),
            P(None, "seq"),
            P(None, "seq"),
            P("seq", None),
            P(None, "seq"),
            P(None, "seq"),
            P("seq", None),
            P(),
            P(),
            P("seq"),
            P("batch", "seq", None),
        ),
        out_specs=(
            P("batch", "seq", None),
            P("batch", "seq", None),
            P(None, "seq"),
            P(None, "seq"),
            P(None, "seq"),
            P(None, "seq"),
            P("seq", None),
            P(None, "seq"),
            P(None, "seq"),
            P("seq", None),
            P(),
            P(),
            P("seq"),
        ),
        check_vma=False,
    )
```

profile of v0, /device:TPU:0, one launch (start us, length us, event | category | flops | bytes accessed | tf_op | source)
XLA Modules:
  0.0 1104.4 jit_solution(18258999022776441188)
XLA Ops:
  15.8 46.3 %all-gather.5.cloned.1.call-done = bf16[1024,3,1024]{2,0,1:T(8,128)(2,1)} async-done(((bf16[256,3,1024]{2,0,1:T(8,128)(2,1)}), bf16[1024,3,1024]{2,0,1:T(8,128)(2,1)}) %all-gather.5.cloned.1.call-update) | async-done | bytes 6291472 | tf_op jit(solution)/shard_map/all_gather | solution.py:100
  62.1 8.9 fusion.88
  77.7 35.9 %while.24 = (s32[]{:T(128)}, f32[3,1024,4,64]{1,3,2,0:T(8,128)}, bf16[3,1024,4,64]{1,3,2,0:T(8,128)(2,1)}, bf16[3,1024,4,64]{1,3,2,0:T(8,128)(2,1)}, bf16[3,1024,4,64]{1,3,2,0:T(8,128)(2,1)}, /*index=5*/s32[]{:T(128)}) while((s32[]{:T(128)}, f32[3,1024,4,64]{1,3,2,0:T(8,128)}, bf16[3,1024,4,64]{1,3,2,0:T(8,128)(2,1)}, ...), condition=%wide.region_3.4_spmd, body=%wide.region_2.3_spmd.sunk | while | flops 1083179008 | bytes 9962577 | solution.py:126
  82.2 7.5 fusion.135
  94.1 7.5 fusion.135
  106.0 7.5 fusion.135
  128.4 57.7 %reduce-scatter.5.cloned.1.call-done = bf16[256,3,1024]{2,0,1:T(8,128)(2,1)} async-done(((bf16[1024,3,1024]{2,0,1:T(8,128)(2,1)}), bf16[256,3,1024]{2,0,1:T(8,128)(2,1)}) %reduce-scatter.5.cloned.1.call-update) | async-done | bytes 1572880 | tf_op jit(solution)/shard_map/reduce_scatter | solution.py:132
  190.1 44.1 %all-gather.9.cloned.1.call-done = bf16[1024,3,1024]{2,0,1:T(8,128)(2,1)} async-done(((bf16[256,3,1024]{2,0,1:T(8,128)(2,1)}), bf16[1024,3,1024]{2,0,1:T(8,128)(2,1)}) %all-gather.9.cloned.1.call-update) | async-done | bytes 6291472 | tf_op jit(solution)/shard_map/all_gather | solution.py:145
  234.2 9.9 convolution_convert_fusion.5
  244.1 38.5 %all-gather.7.cloned.1.call-done = bf16[1024,3,1024]{2,0,1:T(8,128)(2,1)} async-done(((bf16[256,3,1024]{2,0,1:T(8,128)(2,1)}), bf16[1024,3,1024]{2,0,1:T(8,128)(2,1)}) %all-gather.7.cloned.1.call-update) | async-done | bytes 6291472 | tf_op jit(solution)/shard_map/all_gather | solution.py:136
  282.7 7.8 fusion.81
  290.5 8.3 fusion.83
  298.8 9.0 multiply_convert_fusion
  311.2 11.9 %add_convert_fusion = bf16[1024,3,1024]{2,0,1:T(8,128)(2,1)} fusion(f32[1024,3,1024]{2,0,1:T(8,128)} %fusion.83, bf16[1024,704]{0,1:T(8,128)(2,1)} %param.28, f32[1024,3,704]{0,2,1:T(8,128)S(1)} %get-tuple-element.155, bf16[1024,3,704]{0,2,1:T(8,128)(2,1)} %convolution_convert_fusion.5), kind=kOutput, calls=%fused_computation.45 | convolution fusion | flops 4441964544 | bytes 33292288 | tf_op jit(solution)/shard_map/dot_general | solution.py:34
  323.3 58.3 %reduce-scatter.9.cloned.1.call-done = bf16[256,3,1024]{2,0,1:T(8,128)(2,1)} async-done(((bf16[1024,3,1024]{2,0,1:T(8,128)(2,1)}), bf16[256,3,1024]{2,0,1:T(8,128)(2,1)}) %reduce-scatter.9.cloned.1.call-update) | async-done | bytes 1572880 | tf_op jit(solution)/shard_map/reduce_scatter | solution.py:152
  390.2 46.5 %all-gather.11.cloned.1.call-done = bf16[1024,3,1024]{2,0,1:T(8,128)(2,1)} async-done(((bf16[256,3,1024]{2,0,1:T(8,128)(2,1)}), bf16[1024,3,1024]{2,0,1:T(8,128)(2,1)}) %all-gather.11.cloned.1.call-update) | async-done | bytes 6291472 | tf_op jit(solution)/shard_map/all_gather | solution.py:164
  436.6 8.5 convert_multiply_fusion.5
  448.9 52.2 %while.25 = (s32[]{:T(128)}, bf16[3,1024,4,64]{1,3,2,0:T(8,128)(2,1)}, bf16[3,1024,4,64]{1,3,2,0:T(8,128)(2,1)}, bf16[3,1024,4,64]{1,3,2,0:T(8,128)(2,1)}, bf16[...) while((s32[]{:T(128)}, ...), condition=%wide.region_12.13_spmd, body=%wide.region_11.12_spmd.sunk | while | flops 2702966784 | bytes 33559652 | solution.py:174
  449.4 6.2 fusion.147
  466.7 6.2 fusion.147
  484.0 6.2 fusion.147
  507.2 9.4 convolution_convert_fusion.4
  516.6 9.3 convolution_convert_fusion.2
  526.0 11.4 %convolution_bitcast_fusion.3 = f32[704,1024]{1,0:T(8,128)} fusion(bf16[1024,3,704]{0,2,1:T(8,128)(2,1)} %get-tuple-element.154, bf16[1024,3,1024]{2,0,1:T(8,128)(2,1)} %all-gather.9.cloned.1.call-done), kind=kOutput, calls=%fused_computation.115 | convolution fusion | flops 4429185024 | bytes 13500416 | tf_op jit(solution)/shard_map/dot_general | solution.py:43
  537.5 13.4 %convolution_bitcast_fusion.2 = f32[1024,704]{0,1:T(8,128)} fusion(bf16[1024,3,1024]{2,0,1:T(8,128)(2,1)} %all-gather.7.cloned.1.call-done, f32[1024,3,704]{0,2,1:T(8,128)} %copy-done.13, bf16[1024,3,704]{0,2,1:T(8,128)(2,1)} %convolution_convert_fusion.5), kind=kOutput, calls=%fused_computation.114 | convolution fusion | flops 4435673088 | bytes 22151168 | tf_op jit(solution)/shard_map/dot_general | solution.py:43
  551.0 8.8 convolution_bitcast_fusion.1
  559.7 9.2 convolution_bitcast_fusion
  571.2 5.5 convolution_bitcast_fusion.4
  576.9 22.3 %psum.87 = f32[256]{0:T(256)} all-reduce(f32[256]{0:T(256)S(1)} %reshape.129), channel_id=1, replica_groups=mesh['batch'=8,'seq'=4] {'batch'}, use_global_device_ids=true, to_apply=%region_28.29 | all-reduce | flops 256 | bytes 2048 | tf_op jit(solution)/shard_map/psum | solution.py:211
  602.2 37.4 %all-reduce = (f32[1024]{0:T(1024)}, f32[1024]{0:T(1024)}) all-reduce(f32[1024]{0:T(1024)S(1)} %get-tuple-element.102, f32[1024]{0:T(1024)S(1)} %copy-done.47), channel_id=1, replica_groups=mesh['batch'=8,'seq'=4] {'batch','seq'}, use_global_device_ids=true, to_apply=%region_24.25 | all-reduce | flops 2048 | bytes 16384 | tf_op jit(solution)/shard_map/psum | solution.py:196
  639.6 6.1 fusion.52
  645.7 437.0 %all-reduce.4.cloned.1.call-done = (f32[1024,256]{1,0:T(8,128)}, f32[1024,256]{1,0:T(8,128)}, f32[1024,256]{1,0:T(8,128)}, f32[1024,256]{1,0:T(8,128)}, f32[256,...) async-done(((f32[1024,256]{1,0:T(8,128)}, f32[1024,256]{1,0:T(8,128)}, f32[1024,256]{1,0:T(8,128)}, f32[1024,256]{1,0:T(8,128)}, ...) | async-done | bytes 13893648 | tf_op jit(solution)/shard_map/psum | solution.py:211
  (212 shorter events, 122.5 us)
Async XLA Ops:
  7.2 283.3 %copy-start = (bf16[1024,704]{0,1:T(8,128)(2,1)S(1)}, bf16[1024,704]{0,1:T(8,128)(2,1)}, u32[]{:S(2)}) copy-start(bf16[1024,704]{0,1:T(8,128)(2,1)} %param.27) | copy-start | bytes 4325380
  7.2 54.9 %all-gather.5.cloned.1.call-start = ((), (), s32[]{:S(2)}) async-start(), calls=%async_computation.4 | async-start | bytes 7864320 | tf_op jit(solution)/shard_map/all_gather | solution.py:100
  12.9 173.2 %reduce-scatter.5.cloned.1.call-start = ((), (), s32[]{:S(2)}) async-start(), calls=%async_computation.5 | async-start | bytes 7864320 | tf_op jit(solution)/shard_map/reduce_scatter | solution.py:132
  14.0 48.1 %copy-start.29 = (bf16[1024,256]{0,1:T(8,128)(2,1)S(1)}, bf16[1024,256]{0,1:T(8,128)(2,1)}, u32[]{:S(2)}) copy-start(bf16[1024,256]{0,1:T(8,128)(2,1)} %copy.39) | copy-start | bytes 1572868
  15.2 55.8 %copy-start.32 = (bf16[1024,256]{0,1:T(8,128)(2,1)}, bf16[1024,256]{0,1:T(8,128)(2,1)S(1)}, u32[]{:S(2)}) copy-start(bf16[1024,256]{0,1:T(8,128)(2,1)S(1)} %copy.41) | copy-start | bytes 1572868
  15.5 55.6 %copy-start.34 = (bf16[1024,256]{0,1:T(8,128)(2,1)}, bf16[1024,256]{0,1:T(8,128)(2,1)S(1)}, u32[]{:S(2)}) copy-start(bf16[1024,256]{0,1:T(8,128)(2,1)S(1)} %copy.42) | copy-start | bytes 1572868
  15.8 56.9 %copy-start.36 = (f32[1024,3]{0,1:T(4,128)}, f32[1024,3]{0,1:T(4,128)S(1)}, u32[]{:S(2)}) copy-start(f32[1024,3]{0,1:T(4,128)S(1)} %fusion.91) | copy-start | bytes 36868
  127.6 58.5 %copy-start.2 = (bf16[3,256,1024]{2,1,0:T(8,128)(2,1)S(1)}, bf16[3,256,1024]{2,1,0:T(8,128)(2,1)}, u32[]{:S(2)}) copy-start(bf16[3,256,1024]{2,1,0:T(8,128)(2,1)} %param.19) | copy-start | bytes 4718596
  127.6 60.6 %copy-start.40 = (f32[1024]{0:T(1024)S(1)}, f32[1024]{0:T(1024)}, u32[]{:S(2)}) copy-start(f32[1024]{0:T(1024)} %param.31) | copy-start | bytes 12292
  127.6 106.6 %all-gather.9.cloned.1.call-start = ((), (), s32[]{:S(2)}) async-start(), calls=%async_computation.8 | async-start | bytes 7864320 | tf_op jit(solution)/shard_map/all_gather | solution.py:145
  128.3 154.3 %all-gather.7.cloned.1.call-start = ((), (), s32[]{:S(2)}) async-start(), calls=%async_computation.6 | async-start | bytes 7864320 | tf_op jit(solution)/shard_map/all_gather | solution.py:136
  188.2 197.5 %copy-start.38 = (f32[256,3]{0,1:T(4,128)}, f32[256,3]{0,1:T(4,128)S(1)}, u32[]{:S(2)}) copy-start(f32[256,3]{0,1:T(4,128)S(1)} %add_rsqrt_fusion.1) | copy-start | bytes 9220
  190.0 191.6 %reduce-scatter.9.cloned.1.call-start = ((), (), s32[]{:S(2)}) async-start(), calls=%async_computation.9 | async-start | bytes 7864320 | tf_op jit(solution)/shard_map/reduce_scatter | solution.py:152
  323.1 113.5 %all-gather.11.cloned.1.call-start = ((), (), s32[]{:S(2)}) async-start(), calls=%async_computation.10 | async-start | bytes 7864320 | tf_op jit(solution)/shard_map/all_gather | solution.py:164
  385.7 50.9 %copy-start.24 = (bf16[256,1024]{1,0:T(8,128)(2,1)S(1)}, bf16[256,1024]{1,0:T(8,128)(2,1)}, u32[]{:S(2)}) copy-start(bf16[256,1024]{1,0:T(8,128)(2,1)} %param.26) | copy-start | bytes 1572868
  390.1 209.1 %reduce-scatter.11.cloned.1.call-start = ((), (), s32[]{:S(2)}) async-start(), calls=%async_computation.11 | async-start | bytes 7864320 | tf_op jit(solution)/shard_map/reduce_scatter | solution.py:189
  448.9 52.2 %copy-start.37 = (f32[1024,3]{0,1:T(4,128)S(1)}, f32[1024,3]{0,1:T(4,128)}, u32[]{:S(2)}) copy-start(f32[1024,3]{0,1:T(4,128)} %copy-done.36) | copy-start | bytes 36868
  516.6 123.0 %reduce-scatter.7.cloned.1.call-start = ((), (), s32[]{:S(2)}) async-start(), calls=%async_computation.7 | async-start | bytes 7864320 | tf_op jit(solution)/shard_map/reduce_scatter | solution.py:140
  525.9 556.8 %all-reduce.4.cloned.1.call-start = ((), (), s32[]{:S(2)}) async-start(), calls=%async_computation.12 | async-start | bytes 27787264 | tf_op jit(solution)/shard_map/psum | solution.py:211
  526.0 24.9 %slice-start = ((s8[8650752]{0:T(1024)(128)(4,1)}), s8[4194304]{0:T(1024)(128)(4,1)S(1)}, s32[]{:S(2)}) async-start(s8[8650752]{0:T(1024)(128)(4,1)} %bitcast.238), calls=%async_computation.13 | async-start | bytes 8388608
  526.0 24.9 %slice-start.1 = ((s8[8650752]{0:T(1024)(128)(4,1)}), s8[4194304]{0:T(1024)(128)(4,1)S(1)}, s32[]{:S(2)}) async-start(s8[8650752]{0:T(1024)(128)(4,1)} %bitcast.238), calls=%async_computation.14 | async-start | bytes 8388608
  526.0 24.9 %slice-start.3 = ((s8[6291456]{0:T(1024)(128)(4,1)}), s8[4194304]{0:T(1024)(128)(4,1)S(1)}, s32[]{:S(2)}) async-start(s8[6291456]{0:T(1024)(128)(4,1)} %bitcast.240), calls=%async_computation.16 | async-start | bytes 8388608
  537.4 13.5 %slice-start.2 = ((s8[8650752]{0:T(1024)(128)(4,1)}), s8[262144]{0:T(1024)(128)(4,1)S(1)}, s32[]{:S(2)}) async-start(s8[8650752]{0:T(1024)(128)(4,1)} %bitcast.238), calls=%async_computation.15 | async-start | bytes 524288
  537.5 13.5 %slice-start.4 = ((s8[6291456]{0:T(1024)(128)(4,1)}), s8[2097152]{0:T(1024)(128)(4,1)S(1)}, s32[]{:S(2)}) async-start(s8[6291456]{0:T(1024)(128)(4,1)} %bitcast.240), calls=%async_computation.17 | async-start | bytes 4194304
  537.5 22.3 %slice-start.5 = ((s8[6291456]{0:T(1024)(128)(4,1)}), s8[4194304]{0:T(1024)(128)(4,1)S(1)}, s32[]{:S(2)}) async-start(s8[6291456]{0:T(1024)(128)(4,1)} %bitcast.243), calls=%async_computation.18 | async-start | bytes 8388608
  576.8 22.4 %copy-start.3 = (bf16[3,256,1024]{2,1,0:T(8,128)(2,1)S(1)}, bf16[3,256,1024]{2,1,0:T(8,128)(2,1)}, u32[]{:S(2)}) copy-start(bf16[3,256,1024]{2,1,0:T(8,128)(2,1)} %param.19) | copy-start | bytes 4718596
  576.8 22.4 %copy-start.43 = (f32[256,3]{0,1:T(4,128)S(1)}, f32[256,3]{0,1:T(4,128)}, u32[]{:S(2)}) copy-start(f32[256,3]{0,1:T(4,128)} %copy-done.42) | copy-start | bytes 9220
  576.8 22.4 %copy-start.44 = (f32[1024]{0:T(1024)S(1)}, f32[1024]{0:T(1024)}, u32[]{:S(2)}) copy-start(f32[1024]{0:T(1024)} %param.30) | copy-start | bytes 12292
  576.8 25.4 %copy-start.47 = (f32[1024]{0:T(1024)S(1)}, f32[1024]{0:T(1024)}, u32[]{:S(2)}) copy-start(f32[1024]{0:T(1024)} %get-tuple-element.98) | copy-start | bytes 12292
  576.8 62.8 %copy-start.39 = (f32[256,3]{0,1:T(4,128)S(1)}, f32[256,3]{0,1:T(4,128)}, u32[]{:S(2)}) copy-start(f32[256,3]{0,1:T(4,128)} %copy-done.38) | copy-start | bytes 9220
  576.8 62.8 %copy-start.41 = (f32[1024]{0:T(1024)S(1)}, f32[1024]{0:T(1024)}, u32[]{:S(2)}) copy-start(f32[1024]{0:T(1024)} %param.31) | copy-start | bytes 12292
  576.8 62.8 %copy-start.46 = (f32[256,3]{0,1:T(4,128)S(1)}, f32[256,3]{0,1:T(4,128)}, u32[]{:S(2)}) copy-start(f32[256,3]{0,1:T(4,128)} %copy-done.45) | copy-start | bytes 9220
  (38 other events, 172.5 us)
Sparse Core Ops, SparseCore 0:
  13.0 49.0 all-gather.4
  127.7 58.3 reduce-scatter.4
  187.7 46.3 all-gather.8
  236.2 46.3 all-gather.6
  323.2 58.3 reduce-scatter.8
  390.2 46.3 all-gather.10
  516.7 58.3 reduce-scatter.10
  577.8 59.2 reduce-scatter.6
  643.9 438.7 all-reduce.3
where the time goes:
time: 1110 us; the launch traced here: 1100 us
  waiting for transfers between devices  729 us (66%)
  matrix products  209 us (19%)
  blocking collectives  59.7 us (5%)
  other arithmetic  48.2 us (4%)
  local copies, waits for them, and re-layouts  42.2 us (4%)
  between operations  14.6 us (1%)
    psum x1, waiting for transfers between devices, on_device(): lax.psum((grad_qw, grad_kw, grad_vw, grad_gw, grad_outw, grad_upw, grad_p...  437 us
    reduce_scatter x1, waiting for transfers between devices, on_device(): lax.psum_scatter((matmul_back(grad_up, up_weight) + matmul_back(grad_pair...  58.3 us
    reduce_scatter x1, waiting for transfers between devices, on_device(): lax.psum_scatter(matmul(gated, out_weight).astype(jnp.bfloat16), 'seq', s...  57.7 us
    dot_general x5, matrix products, weight_grad(): lax.dot_general(inputs, grads, (((0, 1), (0, 1)), ((), ())), preferred_el...  48.4 us
    dot_general x5, matrix products, matmul_back(): lax.dot_general(left_operand, right_operand, (((left_operand.ndim - 1,),...  48 us
    all_gather x1, waiting for transfers between devices, on_device(): lax.all_gather(grad_middle.astype(jnp.bfloat16), 'seq', axis=0, tiled=True)  46.5 us
    all_gather x1, waiting for transfers between devices, on_device(): lax.all_gather(scaled_one.astype(jnp.bfloat16), 'seq', axis=0, tiled=True)  46.3 us
    all_gather x1, waiting for transfers between devices, on_device(): grad_full = lax.all_gather(grad_local_part, 'seq', axis=0, tiled=True)  44.1 us
  transfers between devices with their start and end apart: 9, of which 7 were waited for; matrix products, arithmetic and copies ran while one was open for 8% of the time, Pallas kernels for 0%

commit v1 on v0

v1 whole, which is shorter than its diff:
```python
import functools

import jax
import jax.numpy as jnp
from jax import lax
from jax.experimental import pallas as pl
from jax.experimental.pallas import tpu as pltpu
from jax.sharding import PartitionSpec as P

HD = 64
EPS = 1e-05
BF = jnp.bfloat16
F32 = jnp.float32
VMEM_LIMIT = 62 * 1024 * 1024
MESH = pl.DeviceIdType.MESH
BLOCKS = 4


def nn(a, b):
    return lax.dot_general(a, b, (((1,), (0,)), ((), ())), preferred_element_type=F32)


def nt(a, b):
    return lax.dot_general(a, b, (((1,), (1,)), ((), ())), preferred_element_type=F32)


def tn(a, b):
    return lax.dot_general(a, b, (((0,), (0,)), ((), ())), preferred_element_type=F32)


def same_head(width):
    rows = lax.broadcasted_iota(jnp.int32, (width, width), 0) // HD
    cols = lax.broadcasted_iota(jnp.int32, (width, width), 1) // HD
    return rows == cols


def by_head(array):
    rows, width = array.shape
    lane = lax.broadcasted_iota(jnp.int32, (rows, width), 1) // HD
    zero = jnp.zeros_like(array)
    return jnp.concatenate([jnp.where(lane == h, array, zero) for h in range(width // HD)], axis=0)


def causal(rows, heads, transposed):
    one = lax.broadcasted_iota(jnp.int32, (rows, rows), 0)
    two = lax.broadcasted_iota(jnp.int32, (rows, rows), 1)
    keep = (two >= one) if transposed else (one >= two)
    return jnp.concatenate([keep] * heads, axis=1)


def masked(scores, keep):
    return jnp.where(keep, scores, 0.0).astype(BF)


def head_mean(array, ones):
    return nn(array.astype(BF), ones) * (1.0 / HD)


def softplus(v):
    return jnp.maximum(v, 0.0) + jnp.log1p(jnp.exp(-jnp.abs(v)))


def sigmoid_of_softplus(q):
    series = q * (1.0 - q * (0.5 - q * (1.0 / 6.0)))
    return jnp.where(q < 0.03, series, 1.0 - jnp.exp(-q))


def sigmoid(v):
    return 1.0 / (1.0 + jnp.exp(-v))


class Peers:
    def __init__(self, batch=1):
        self.place = lax.axis_index("seq")
        self.group = lax.axis_index("batch")
        self.chip, self.core = self.place // 2, self.place % 2
        self.across = (self.group, (1 - self.chip) * 2 + self.core)
        self.beside = (self.group, self.chip * 2 + 1 - self.core)
        self.hops = batch.bit_length() - 1

    def bit(self, h):
        return (self.group // 2**h) % 2

    def partner(self, h):
        return (self.group + (1 - 2 * self.bit(h)) * 2**h, self.place)

    def meet(self):
        others = [self.across, self.beside] + [self.partner(h) for h in range(self.hops)]
        barrier = pltpu.get_barrier_semaphore()
        for peer in others:
            pl.semaphore_signal(barrier, inc=1, device_id=peer, device_id_type=MESH)
        pl.semaphore_wait(barrier, len(others))

    def relative(self, index):
        return ((index // 2 + self.chip) % 2) * 2 + (index % 2 + self.core) % 2


def spot(j):
    return (j % 2) * 2 + j // 2


def remote(source, target, sems, index, peer):
    send, recv = sems
    return pltpu.make_async_remote_copy(
        src_ref=source,
        dst_ref=target,
        send_sem=send.at[index],
        recv_sem=recv.at[index],
        device_id=peer,
        device_id_type=MESH,
    )


class Gather:
    def __init__(self, peers, buffer, sems, own=None):
        self.peers, self.buffer, self.sems = peers, buffer, sems
        self.own = own or (lambda k: buffer.at[k, 0])

    def chip_hop(self, k):
        return remote(self.own(k), self.buffer.at[k, 2], self.sems, 3 * k, self.peers.across)

    def core_hop(self, k):
        return remote(self.own(k), self.buffer.at[k, 1], self.sems, 3 * k + 1, self.peers.beside)

    def passed_on(self, k):
        return remote(
            self.buffer.at[k, 2], self.buffer.at[k, 3], self.sems, 3 * k + 2, self.peers.beside
        )

    def start(self, k):
        self.chip_hop(k).start()
        self.core_hop(k).start()

    def forward(self, k):
        self.chip_hop(k).wait_recv()
        self.passed_on(k).start()

    def arrived(self, k):
        self.core_hop(k).wait_recv()
        self.passed_on(k).wait_recv()

    def sent(self, k):
        self.chip_hop(k).wait_send()
        self.core_hop(k).wait_send()
        self.passed_on(k).wait_send()


class Scatter:
    def __init__(self, peers, pair, middle, came, far, sems):
        self.peers, self.pair, self.middle = peers, pair, middle
        self.came, self.far, self.sems = came, far, sems

    def core_hop(self, k):
        return remote(self.pair(k), self.came.at[k], self.sems, 2 * k, self.peers.beside)

    def chip_hop(self, k):
        return remote(self.middle(k), self.far.at[k], self.sems, 2 * k + 1, self.peers.across)

    def start(self, k):
        self.core_hop(k).start()

    def middle_step(self, k):
        self.core_hop(k).wait_recv()
        middle = self.middle(k)

        def add(rows):
            middle[rows] = (middle[rows].astype(F32) + self.came[k, 1, rows].astype(F32)).astype(BF)

        by_rows(middle.shape[0], add)
        self.chip_hop(k).start()

    def arrived(self, k):
        self.chip_hop(k).wait_recv()

    def sent(self, k):
        self.core_hop(k).wait_send()
        self.chip_hop(k).wait_send()


class Reduce:
    def __init__(self, peers, bits, send, work, came, total, sems, local):
        self.peers, self.send, self.work, self.came, self.total = peers, send, work, came, total
        self.sems, self.local = sems, local
        self.bits = bits
        self.extra = [h for h in range(peers.hops) if h not in bits]
        self.b = [peers.bit(h) for h in bits]
        b0, b1, b2 = self.b
        self.kept = b1 * 2 + b2
        self.piece = b0 * 4 + self.kept
        self.stage = 0

    def hop(self, t):
        _, b1, b2 = self.b
        if t == 0:
            source, target = self.send, self.came.at[pl.ds(0, 4)]
        elif t == 1:
            source, target = self.work.at[pl.ds((1 - b1) * 2, 2)], self.came.at[pl.ds(4, 2)]
        elif t == 2:
            source, target = self.work.at[pl.ds(b1 * 2 + 1 - b2, 1)], self.came.at[pl.ds(6, 1)]
        else:
            source, target = self.work.at[pl.ds(self.kept, 1)], self.came.at[pl.ds(4 + t, 1)]
        h = (list(self.bits) + self.extra)[t]
        return remote(source, target, self.sems, t, self.peers.partner(h))

    def back(self, t):
        b0, b1, _ = self.b
        where = (pl.ds(b0 * 4, 4), pl.ds(b0 * 4 + b1 * 2, 2), pl.ds(self.piece, 1))[t]
        source = self.work.at[pl.ds(self.kept, 1)] if t == 2 else self.total.at[where]
        index = 3 + len(self.extra) + t
        return remote(
            source, self.total.at[where], self.sems, index, self.peers.partner(self.bits[t])
        )

    def own(self):
        where = pl.ds(self.piece, 1)
        return pltpu.make_async_copy(
            self.work.at[pl.ds(self.kept, 1)], self.total.at[where], self.local
        )

    def begin(self):
        self.hop(0).start()

    def step(self, stage=None):
        t, last = self.stage if stage is None else stage, 3 + len(self.extra)
        self.stage = max(self.stage, t + 1)
        if t < last:
            _, b1, _ = self.b
            self.hop(t).wait_recv()
            if t > 2:
                self.hop(t).wait_send()
            base, first, count = (
                (0, 0, 4) if t == 0 else (b1 * 2, 4, 2) if t == 1 else (self.kept, 4 + t, 1)
            )

            def add(q):
                self.work[base + q] = (
                    self.work[base + q].astype(F32) + self.came[first + q].astype(F32)
                ).astype(BF)

            loop(count, add)
            if t + 1 < last:
                self.hop(t + 1).start()
            else:
                self.own().start()
                self.back(2).start()
        else:
            level = 2 - (t - last)
            self.back(level).wait_recv()
            if level == 2:
                self.own().wait()
            if level > 0:
                self.back(level - 1).start()

    def steps(self):
        return 6 + len(self.extra)

    def sent(self):
        for t in range(3):
            self.hop(t).wait_send()
            self.back(t).wait_send()


def by_rows(rows, fn, step=64):
    def one(r, carry):
        fn(pl.ds(pl.multiple_of(r * step, step), step))
        return carry

    lax.fori_loop(0, rows // step, one, 0)


def loop(count, fn):
    def one(k, carry):
        fn(k)
        return carry

    lax.fori_loop(0, count, one, 0)


def normalize(values, gain):
    scale = lax.rsqrt(jnp.mean(values * values, axis=-1, keepdims=True) + EPS)
    normed = values * scale
    return normed, scale, (normed * gain).astype(BF)


def norm_back(grad_out, normed, scale, gain):
    grad_normed = grad_out * gain
    inner = jnp.mean(grad_normed * normed, axis=-1, keepdims=True)
    return scale * (grad_normed - normed * inner)


def forward_kernel(
    length_ref, tokens, cotangent, wq, wk, wv, wg, wo, up, pair, down, gain_one, gain_two, gain_head,
    h1_out, qkvg_out, mixed_out, gated_out, state_out, g_out, res_out, middle_out, gmid_out, sums_out,
    gain_out,
    tok, w4, wo_v, up_v, pair_v, down_v, h1, h2, part, came, far, middle, gmid, state,
    load_sem, save_sem, gload_sem, h1_send, h1_recv, h2_send, h2_recv, g_send, g_recv,
    a_send, a_recv, b_send, b_recv,
):
    slots, rows, feat = tok.shape
    width, hid, wide = wo_v.shape[0], down.shape[0], down_v.shape[0]
    heads = width // HD
    peers = Peers()

    def load(source, target, index):
        return pltpu.make_async_copy(source, target, load_sem.at[index])

    real = pl.ds(0, hid)
    loads = [
        load(tokens, tok, 0),
        *(load(w, w4.at[m], 1 + m) for m, w in enumerate((wq, wk, wv, wg))),
        load(wo, wo_v, 5),
        load(up, up_v.at[real], 6),
        load(pair, pair_v.at[real], 7),
        load(down, down_v.at[real], 8),
        load(cotangent, g_out.at[:, 0], 9),
    ]
    for one in loads:
        one.start()
    peers.meet()
    first = Gather(peers, h1, (h1_send, h1_recv))
    second = Gather(peers, h2, (h2_send, h2_recv))
    grads = Gather(peers, g_out, (g_send, g_recv), lambda k: cotangent.at[k])
    buffers = (lambda k: part.at[k, pl.ds(2, 2)], lambda k: part.at[k, 1], came, far)
    scatter_a = Scatter(peers, *buffers, (a_send, a_recv))
    scatter_b = Scatter(peers, *buffers, (b_send, b_recv))
    g1, g2, gh = gain_one[...], gain_two[...], gain_head[...]

    loads[0].wait()

    def norm_first(k):
        def some(r):
            _, _, hidden = normalize(tok[k, r].astype(F32), g1)
            h1[k, 0, r] = hidden

        by_rows(rows, some)
        first.start(k)

    loop(slots, norm_first)
    loop(slots, lambda k: grads.core_hop(k).start())
    for target in (up_v, pair_v, down_v):
        target[hid:] = jnp.zeros((wide - hid, feat), BF)
    for one in loads[1:6]:
        one.wait()

    block = same_head(width)
    ones = block.astype(BF)

    def attend_all(qkvg, mixed_s, gated_s, state_s):
        def saves(k):
            return [
                pltpu.make_async_copy(qkvg, qkvg_out.at[k], save_sem.at[0]),
                pltpu.make_async_copy(mixed_s, mixed_out.at[k], save_sem.at[1]),
                pltpu.make_async_copy(gated_s, gated_out.at[k], save_sem.at[2]),
                pltpu.make_async_copy(state_s, state_out.at[k], save_sem.at[3]),
            ]

        def attend(k):
            first.forward(k)

            @pl.when(k == 1)
            def _():
                scatter_a.middle_step(0)
                grads.chip_hop(0).start()

            @pl.when(k > 0)
            def _():
                for one in saves(k - 1):
                    one.wait()

            first.arrived(k)
            state[...] = jnp.zeros_like(state)
            length = length_ref[k]

            def chunk(i):
                j = peers.relative(i)
                hidden = h1[k, j]
                position = lax.broadcasted_iota(jnp.int32, (rows, width), 0) + i * rows
                query = softplus(nn(hidden, w4[0])).astype(BF)
                keys = jnp.where(position < length, softplus(nn(hidden, w4[1])), 0.0).astype(BF)
                values = nn(hidden, w4[2]).astype(BF)
                gate = nn(hidden, w4[3])
                qkvg[j, 0] = query
                qkvg[j, 1] = keys
                qkvg[j, 2] = values
                qkvg[j, 3] = gate.astype(BF)
                before = state[...].astype(BF)
                state_s[i] = before
                scores = masked(nt(query, by_head(keys)), causal(rows, heads, False))
                mixed = nn(query, before) + nn(scores, by_head(values))
                state[...] += jnp.where(block, tn(keys, values), 0.0)
                mixed_s[j] = mixed.astype(BF)
                scale = lax.rsqrt(head_mean(mixed * mixed, ones) + EPS)
                gated_s[j] = (mixed * scale * gh * (gate * sigmoid(gate))).astype(BF)

            loop(BLOCKS, chunk)
            for one in saves(k):
                one.start()

            def project(p):
                j = (p % 2) * 2 + p // 2
                part[k, p] = nn(gated_s[j], wo_v[...]).astype(BF)

            project(2)
            project(3)
            scatter_a.start(k)
            project(1)
            project(0)

        loop(slots, attend)
        for one in saves(slots - 1):
            one.wait()

    v = pltpu.VMEM
    pl.run_scoped(
        attend_all,
        v((BLOCKS, 4, rows, width), BF),
        v((BLOCKS, rows, width), BF),
        v((BLOCKS, rows, width), BF),
        v((BLOCKS, width, width), BF),
    )

    def finish_attend(k):
        scatter_a.arrived(k)

        def some(r):
            value = (
                tok[k, r].astype(F32)
                + part[k, 0, r].astype(F32)
                + came[k, 0, r].astype(F32)
                + far[k, r].astype(F32)
            )
            middle[k, r] = value
            _, _, hidden = normalize(value, g2)
            h2[k, 0, r] = hidden

        by_rows(rows, some)
        second.start(k)
        scatter_a.sent(k)

    def follow(k):
        scatter_a.middle_step(k)
        grads.chip_hop(k).start()

    finish_attend(0)
    follow(1)
    h1_save = pltpu.make_async_copy(h1, h1_out, save_sem.at[4])
    h1_save.start()
    for one in loads[6:]:
        one.wait()

    def unit_all(prod_s, gu_s, gp_s, gbuf, res_s, sums, staged):
        def unit_save(k):
            return pltpu.make_async_copy(res_s, res_out.at[k], save_sem.at[9])

        def clear(m):
            sums[m // 3, pl.ds(pl.multiple_of(m % 3 * (wide // 3), wide // 3), wide // 3)] = jnp.zeros(
                (wide // 3, feat), F32
            )

        loop(9, clear)

        def unit(k):
            second.forward(k)
            grads.forward(k)

            @pl.when(k > 0)
            def _():
                unit_save(k - 1).wait()

            second.arrived(k)
            grads.arrived(k)
            for j in range(BLOCKS):
                pltpu.make_async_copy(g_out.at[k, j], gbuf.at[j], gload_sem.at[j]).start()

            def one(t):
                @pl.when((t == 2) & (k + 1 < slots))
                def _():
                    finish_attend(k + 1)

                @pl.when((t == 2) & (k + 2 < slots))
                def _():
                    follow(k + 2)

                j = t + (t // 2) * (1 - 2 * (t % 2))
                pltpu.make_async_copy(g_out.at[k, j], gbuf.at[j], gload_sem.at[j]).wait()
                hidden, grad = h2[k, j], gbuf[j]
                up_part = nt(hidden, up_v[...])
                pair_part = nt(hidden, pair_v[...])
                product = (up_part * pair_part).astype(BF)
                prod_s[j] = product
                res_s[spot(j)] = nn(product, down_v[...]).astype(BF)
                grad_product = nt(grad, down_v[...]).astype(BF).astype(F32)
                grad_up = (grad_product * pair_part).astype(BF)
                grad_pair = (grad_product * up_part).astype(BF)
                gu_s[j] = grad_up
                gp_s[j] = grad_pair
                part[k, spot(j)] = (nn(grad_up, up_v[...]) + nn(grad_pair, pair_v[...])).astype(BF)

                @pl.when(t == 2)
                def _():
                    scatter_b.start(k)

            loop(BLOCKS, one)
            unit_save(k).start()

            @pl.when(k == 1)
            def _():
                scatter_b.middle_step(0)

            @pl.when(k > 0)
            def _():
                scatter_b.middle_step(k)

            hidden_all = h2[k].reshape(BLOCKS * rows, feat)
            grad_all = gbuf[...].reshape(BLOCKS * rows, feat)
            tile = wide // 3

            def weigh(m):
                cols = pl.ds(pl.multiple_of(m * tile, tile), tile)

                def of(ref):
                    return ref[:, :, cols].reshape(BLOCKS * rows, tile)

                sums[0, cols] += tn(of(prod_s), grad_all)
                sums[1, cols] += tn(of(gu_s), hidden_all)
                sums[2, cols] += tn(of(gp_s), hidden_all)

            loop(3, weigh)

        loop(slots, unit)
        eighth = hid // 8

        def sums_save(c):
            return pltpu.make_async_copy(staged, sums_out.at[c], save_sem.at[6])

        for c in range(3):
            if c:
                sums_save(c - 1).wait()

            def convert(p):
                staged[p] = sums[c, pl.ds(pl.multiple_of(p * eighth, 8), eighth)].astype(BF)

            loop(8, convert)
            sums_save(c).start()
        sums_save(2).wait()
        unit_save(slots - 1).wait()

    pl.run_scoped(
        unit_all,
        v((BLOCKS, rows, wide), BF),
        v((BLOCKS, rows, wide), BF),
        v((BLOCKS, rows, wide), BF),
        v((BLOCKS, rows, feat), BF),
        v((BLOCKS, rows, feat), BF),
        v((3, wide, feat), F32),
        v((8, hid // 8, feat), BF),
    )
    middle_save = pltpu.make_async_copy(middle, middle_out, save_sem.at[5])
    middle_save.start()
    own_grads = load(cotangent, tok, 0)
    own_grads.start()
    own_grads.wait()
    gain_out[...] = jnp.zeros_like(gain_out)

    def gmid_save(k):
        return pltpu.make_async_copy(gmid.at[k % 2], gmid_out.at[k], save_sem.at[11 + k % 2])

    def finish_unit(k):
        scatter_b.arrived(k)

        @pl.when(k > 1)
        def _():
            gmid_save(k - 2).wait()

        def some(r):
            grad = (
                part[k, 0, r].astype(F32) + came[k, 0, r].astype(F32) + far[k, r].astype(F32)
            )
            normed, scale, _ = normalize(middle[k, r], g2)
            gain_out[...] += jnp.sum(grad * normed, axis=0, keepdims=True)
            gmid[k % 2, r] = tok[k, r].astype(F32) + norm_back(grad, normed, scale, g2)

        by_rows(rows, some)
        gmid_save(k).start()

    loop(slots, finish_unit)
    for k in range(max(slots - 2, 0), slots):
        gmid_save(k).wait()
    for save in (h1_save, middle_save):
        save.wait()

    def settle(k):
        first.sent(k)
        second.sent(k)
        grads.sent(k)
        scatter_b.sent(k)

    loop(slots, settle)


def dma(n):
    return pltpu.SemaphoreType.DMA((n,))


def anywhere(n):
    return [pl.BlockSpec(memory_space=pl.ANY)] * n


def in_vmem(n):
    return [pl.BlockSpec(memory_space=pltpu.VMEM)] * n


def forward(lengths, tokens, cotangent, q4, wo, up, pair, down, gain_one, gain_two, gain_head):
    slots, rows, feat = tokens.shape
    width, hid = wo.shape[0], down.shape[0]
    n = BLOCKS
    shape = jax.ShapeDtypeStruct
    wide = -(-hid // 256) * 256
    blocks = lambda *dims: shape((slots, n) + dims, BF)
    outs = [
        blocks(rows, feat),
        blocks(4, rows, width),
        blocks(rows, width),
        blocks(rows, width),
        blocks(width, width),
        blocks(rows, feat),
        blocks(rows, feat),
        shape((slots, rows, feat), F32),
        shape((slots, rows, feat), F32),
        shape((3, 8, hid // 8, feat), BF),
        shape((1, feat), F32),
    ]
    v = pltpu.VMEM
    scratch = [
        v((slots, rows, feat), BF),
        v((4, feat, width), BF),
        v((width, feat), BF),
        v((wide, feat), BF),
        v((wide, feat), BF),
        v((wide, feat), BF),
        v((slots, n, rows, feat), BF),
        v((slots, n, rows, feat), BF),
        v((slots, n, rows, feat), BF),
        v((slots, 2, rows, feat), BF),
        v((slots, rows, feat), BF),
        v((slots, rows, feat), F32),
        v((2, rows, feat), F32),
        v((width, width), F32),
        dma(10),
        dma(13),
        dma(n),
        *[dma(3 * slots)] * 6,
        *[dma(2 * slots)] * 4,
    ]
    total = slots * n * rows
    return pl.pallas_call(
        forward_kernel,
        in_specs=[pl.BlockSpec(memory_space=pltpu.SMEM)] + anywhere(10) + in_vmem(3),
        out_specs=anywhere(10) + in_vmem(1),
        out_shape=outs,
        scratch_shapes=scratch,
        compiler_params=pltpu.CompilerParams(
            collective_id=1, has_side_effects=True, vmem_limit_bytes=VMEM_LIMIT
        ),
        cost_estimate=pl.CostEstimate(
            flops=total * (10 * feat * width + 16 * width * width + 18 * feat * hid),
            transcendentals=total * 6 * width,
            bytes_accessed=2 * total * (6 * feat + 3 * hid),
        ),
        name="forward",
    )(lengths, tokens, cotangent, *q4, wo, up, pair, down, gain_one, gain_two, gain_head)


def backward_kernel(
    batch,
    tokens, middle, gmid, res, qkvg_in, mixed_in, state_in, h1_in, gated_in, sums_in,
    wq, wk, wv, wg, wo, gain_one, gain_head, two_part,
    result, grad_tokens, unit_total, qk_total, vg_total, out_total, gains,
    w4, wo_v, gm, part, came, far, res_mid, came2, far2, state,
    unit_work, unit_came, qk_send, qk_work, qk_came, vg_send, vg_work, vg_came,
    out_send, out_work, out_came, gain_came, head_part,
    load_sem, slot_sem, save_sem, unit_sem, local_sem,
    gm_send, gm_recv, a_send, a_recv, r_send, r_recv, gain_send, gain_recv,
    d_send, d_recv, u_send, u_recv, p_send, p_recv, q_send, q_recv, v_send, v_recv, o_send, o_recv,
):
    slots, _, rows, feat = gm.shape
    width = wo_v.shape[0]
    heads = width // HD
    peers = Peers(batch)

    def load(source, target, index):
        return pltpu.make_async_copy(source, target, load_sem.at[index])

    weight_loads = [
        *(load(w, w4.at[m], 1 + m) for m, w in enumerate((wq, wk, wv, wg))),
        load(wo, wo_v, 5),
        load(res.at[:, 1], res_mid, 6),
    ]
    half = peers.bit(0)
    unit_loads = [
        pltpu.make_async_copy(sums_in.at[c, pl.ds(half * 4, 4)], unit_work.at[c], unit_sem.at[c])
        for c in range(3)
    ]
    for one in (*weight_loads, *unit_loads):
        one.start()
    gather = Gather(peers, gm, (gm_send, gm_recv))
    scatter = Scatter(
        peers, lambda k: part.at[k, pl.ds(2, 2)], lambda k: part.at[k, 1], came, far, (a_send, a_recv)
    )
    results = Scatter(
        peers, lambda k: res.at[k, pl.ds(2, 2)], lambda k: res_mid.at[k], came2, far2, (r_send, r_recv)
    )
    unit_sums = [
        Reduce(
            peers, (0, 1, 2), sums_in.at[c, pl.ds((1 - half) * 4, 4)], unit_work.at[c],
            unit_came.at[c], unit_total.at[c], sems, local_sem.at[c],
        )
        for c, sems in enumerate(((d_send, d_recv), (u_send, u_recv), (p_send, p_recv)))
    ]
    down_sum, up_sum, pair_sum = unit_sums
    qk_sum = Reduce(
        peers, (1, 2, 0), qk_send, qk_work, qk_came, qk_total, (q_send, q_recv), local_sem.at[3]
    )
    vg_sum = Reduce(
        peers, (0, 1, 2), vg_send, vg_work, vg_came, vg_total, (v_send, v_recv), local_sem.at[4]
    )
    out_sum = Reduce(
        peers, (0, 1, 2), out_send, out_work, out_came, out_total, (o_send, o_recv), local_sem.at[5]
    )
    g1, gh = gain_one[...], gain_head[...]
    head_part[...] = jnp.zeros_like(head_part)
    gains[...] = jnp.zeros_like(gains)
    gains[1:2] = two_part[...]
    peers.meet()
    for one in unit_sums:
        one.begin()
    v = pltpu.VMEM

    def begin_all(gmv):
        whole = load(gmid, gmv, 0)
        whole.start()
        whole.wait()

        def begin(k):
            def some(r):
                gm[k, 0, r] = gmv[k, r].astype(BF)

            by_rows(rows, some)
            gather.start(k)

        loop(slots, begin)

    pl.run_scoped(begin_all, v((slots, rows, feat), F32))
    loop(slots, results.start)
    for one in weight_loads:
        one.wait()
    for one in unit_loads:
        one.wait()
    block = same_head(width)
    ones = block.astype(BF)

    def attend_all(qkvg, mixed_v, state_v, h1, gated, pre, sums, out_acc):
        def slot_loads(k):
            b = k % 2
            pairs = (
                (qkvg_in, qkvg), (mixed_in, mixed_v), (state_in, state_v), (h1_in, h1), (gated_in, gated)
            )
            return [
                pltpu.make_async_copy(source.at[k], target.at[b], slot_sem.at[5 * b + m])
                for m, (source, target) in enumerate(pairs)
            ]

        for one in slot_loads(0):
            one.start()

        def attend_back(k):
            b = k % 2
            gather.forward(k)

            @pl.when(k > 0)
            def _():
                scatter.middle_step(k - 1)

            @pl.when(k + 1 < slots)
            def _():
                for one in slot_loads(k + 1):
                    one.start()

            for one in slot_loads(k):
                one.wait()
            gather.arrived(k)
            state[...] = jnp.zeros_like(state)

            def chunk(step):
                @pl.when((k == 0) & (step == 2))
                def _():
                    down_sum.step(0)

                @pl.when((k == 1) & (step == 1))
                def _():
                    down_sum.step(2)
                    up_sum.step(1)

                @pl.when((k == 2) & (step == 1))
                def _():
                    down_sum.step(4)
                    up_sum.step(3)
                    pair_sum.step(1)

                i = BLOCKS - 1 - step
                j = peers.relative(i)
                grad_gated = nt(gm[k, j], wo_v[...]).astype(BF).astype(F32)
                query, keys, values = qkvg[b, j, 0], qkvg[b, j, 1], qkvg[b, j, 2]
                gate = qkvg[b, j, 3].astype(F32)
                mixed = mixed_v[b, j].astype(F32)
                scale = lax.rsqrt(head_mean(mixed * mixed, ones) + EPS)
                normed = mixed * scale
                opened = sigmoid(gate)
                grad_gate = grad_gated * (normed * gh) * opened * (1.0 + gate * (1.0 - opened))
                grad_head = grad_gated * (gate * opened)
                head_part[...] += jnp.sum(grad_head * normed, axis=0, keepdims=True)
                scaled = grad_head * gh
                inner = head_mean(scaled * normed, ones)
                grad_mixed = (scale * (scaled - normed * inner)).astype(BF)
                after = state[...].astype(BF)
                before = state_v[b, i]
                lower = causal(rows, heads, False)
                upper = causal(rows, heads, True)
                query_heads = by_head(query)
                mixed_heads = by_head(grad_mixed)
                grad_scores = masked(nt(grad_mixed, by_head(values)), lower)
                grad_query = nt(grad_mixed, before) + nn(grad_scores, by_head(keys))
                grad_scores_t = masked(nt(values, mixed_heads), upper)
                grad_keys = nt(values, after) + nn(grad_scores_t, query_heads)
                scores_t = masked(nt(keys, query_heads), upper)
                grad_values = nn(keys, after) + nn(scores_t, mixed_heads)
                state[...] += jnp.where(block, tn(query, grad_mixed), 0.0)

                rounded = lambda v: v.astype(BF).astype(F32)
                pre_q = (rounded(grad_query) * sigmoid_of_softplus(query.astype(F32))).astype(BF)
                pre_k = (rounded(grad_keys) * sigmoid_of_softplus(keys.astype(F32))).astype(BF)
                pre_v = grad_values.astype(BF)
                pre_g = grad_gate.astype(BF)
                for m, one in enumerate((pre_q, pre_k, pre_v, pre_g)):
                    pre[j, :, m * width : (m + 1) * width] = one
                grad_h = nt(pre_q, w4[0]) + nt(pre_k, w4[1]) + nt(pre_v, w4[2]) + nt(pre_g, w4[3])
                part[k, spot(j)] = grad_h.astype(BF)

            loop(BLOCKS, chunk)
            scatter.start(k)
            results.middle_step(k)

            @pl.when(k == 0)
            def _():
                down_sum.step(1)
                up_sum.step(0)

            @pl.when(k == 1)
            def _():
                down_sum.step(3)
                up_sum.step(2)
                pair_sum.step(0)

            pre_all = pre[...].reshape(BLOCKS * rows, 4 * width)

            def weigh(m):
                cols = pl.ds(pl.multiple_of(m * 256, 256), 256)
                term = tn(h1[b, :, :, cols].reshape(BLOCKS * rows, 256), pre_all)
                sums[cols] = jnp.where(k > 0, sums[cols], 0.0) + term

            loop(feat // 256, weigh)
            term = tn(gated[b].reshape(BLOCKS * rows, width), gm[k].reshape(BLOCKS * rows, feat))
            out_acc[...] = jnp.where(k > 0, out_acc[...], 0.0) + term

        loop(slots, attend_back)
        scatter.middle_step(slots - 1)
        eighth, part_rows = feat // 8, width // 8

        first = peers.bit(1)

        def fill_all(q):
            at = lambda top: pl.ds(pl.multiple_of((top * 4 + q) * eighth, eighth), eighth)
            qk_work[q] = sums[at(first), : 2 * width].astype(BF)
            qk_send[q] = sums[at(1 - first), : 2 * width].astype(BF)
            vg_work[q] = sums[at(half), 2 * width :].astype(BF)
            vg_send[q] = sums[at(1 - half), 2 * width :].astype(BF)
            small = lambda top: pl.ds(
                pl.multiple_of((top * 4 + q) * part_rows, part_rows), part_rows
            )
            out_work[q] = out_acc[small(half)].astype(BF)
            out_send[q] = out_acc[small(1 - half)].astype(BF)

        loop(4, fill_all)
        for one in (vg_sum, out_sum, qk_sum):
            one.begin()

    pl.run_scoped(
        attend_all,
        v((2, BLOCKS, 4, rows, width), BF),
        v((2, BLOCKS, rows, width), BF),
        v((2, BLOCKS, width, width), BF),
        v((2, BLOCKS, rows, feat), BF),
        v((2, BLOCKS, rows, width), BF),
        v((BLOCKS, rows, 4 * width), BF),
        v((feat, 4 * width), F32),
        v((width, feat), F32),
    )

    def finish_all(tok, mid, gmv, kept):
        finals = [
            load(tokens, tok, 1),
            load(middle, mid, 2),
            load(gmid, gmv, 3),
            load(res.at[:, 0], kept, 4),
        ]
        for one in finals:
            one.start()

        def grad_save(k):
            return pltpu.make_async_copy(gmv.at[k], grad_tokens.at[k], save_sem.at[k])

        def result_save(k):
            return pltpu.make_async_copy(tok.at[k], result.at[k], save_sem.at[slots + k])

        def finish(k):
            scatter.arrived(k)

            def some(r):
                grad = (
                    part[k, 0, r].astype(F32) + came[k, 0, r].astype(F32) + far[k, r].astype(F32)
                )
                normed, scale, _ = normalize(tok[k, r].astype(F32), g1)
                gains[0:1] += jnp.sum(grad * normed, axis=0, keepdims=True)
                gmv[k, r] = gmv[k, r] + norm_back(grad, normed, scale, g1)

            by_rows(rows, some)
            grad_save(k).start()

        def finish_result(k):
            results.arrived(k)

            def some(r):
                total = (
                    mid[k, r]
                    + kept[k, r].astype(F32)
                    + came2[k, 0, r].astype(F32)
                    + far2[k, r].astype(F32)
                )
                tok[k, r] = total.astype(BF)

            by_rows(rows, some)
            result_save(k).start()

        up_sum.step()
        pair_sum.step()
        for one in finals:
            one.wait()
        finish(0)
        finish_result(0)
        qk_sum.step()
        pair_sum.step()
        vg_sum.step()
        out_sum.step()
        finish(1)
        finish_result(1)
        qk_sum.step()
        pair_sum.step()
        vg_sum.step()
        out_sum.step()
        up_sum.step()
        qk_sum.step()
        for k in range(2, slots):
            finish(k)
            finish_result(k)
        lane = lax.broadcasted_iota(jnp.int32, (1, BLOCKS * width), 1) // width
        spread = jnp.concatenate([head_part[...]] * BLOCKS, axis=1)
        gains[2:3] = jnp.where(lane == peers.place, spread, 0.0)
        others = [peers.beside, peers.across] + [peers.partner(h) for h in range(peers.hops)]

        def gain_hop(t):
            return remote(gains, gain_came.at[t], (gain_send, gain_recv), t, others[t])

        def gain_step(t):
            gain_hop(t).wait_recv()
            gain_hop(t).wait_send()
            gains[...] += gain_came[t]
            if t + 1 < len(others):
                gain_hop(t + 1).start()

        gain_hop(0).start()
        waiting = [vg_sum, out_sum, pair_sum, qk_sum, up_sum]
        order = [one for _ in range(8) for one in waiting]
        hop = 0
        for one in order:
            if one.stage < one.steps():
                one.step()
                if hop < len(others):
                    gain_step(hop)
                    hop += 1
        while hop < len(others):
            gain_step(hop)
            hop += 1
        for one in (*unit_sums, qk_sum, vg_sum, out_sum):
            while one.stage < one.steps():
                one.step()
        for one in (*unit_sums, qk_sum, vg_sum, out_sum):
            one.sent()

        def settle(k):
            grad_save(k).wait()
            result_save(k).wait()
            gather.sent(k)
            scatter.sent(k)
            results.sent(k)

        loop(slots, settle)

    pl.run_scoped(
        finish_all,
        v((slots, rows, feat), BF),
        v((slots, rows, feat), F32),
        v((slots, rows, feat), F32),
        v((slots, rows, feat), BF),
    )


def backward(batch, tokens, middle, gmid, res, saved, sums, q4, wo, gain_one, gain_head, two_part):
    slots, rows, feat = tokens.shape
    width = wo.shape[0]
    eighth = sums.shape[2]
    n = BLOCKS
    shape = jax.ShapeDtypeStruct
    v = pltpu.VMEM
    outs = [
        shape((slots, rows, feat), BF),
        shape((slots, rows, feat), F32),
        shape(sums.shape, BF),
        shape((8, feat // 8, 2 * width), BF),
        shape((8, feat // 8, 2 * width), BF),
        shape((8, width // 8, feat), BF),
        shape((3, feat), F32),
    ]
    hops = batch.bit_length() - 1
    extra = hops - 3

    def pieces(*dims):
        return [v((4,) + dims, BF), v((4,) + dims, BF), v((7 + extra,) + dims, BF)]

    scratch = [
        v((4, feat, width), BF),
        v((width, feat), BF),
        v((slots, n, rows, feat), BF),
        v((slots, n, rows, feat), BF),
        v((slots, 2, rows, feat), BF),
        v((slots, rows, feat), BF),
        v((slots, rows, feat), BF),
        v((slots, 2, rows, feat), BF),
        v((slots, rows, feat), BF),
        v((width, width), F32),
        v((3, 4, eighth, feat), BF),
        v((3, 7 + extra, eighth, feat), BF),
        *pieces(feat // 8, 2 * width),
        *pieces(feat // 8, 2 * width),
        *pieces(width // 8, feat),
        v((hops + 2, 3, feat), F32),
        v((1, width), F32),
        dma(7),
        dma(10),
        dma(2 * slots),
        dma(3),
        dma(6),
        *[dma(3 * slots)] * 2,
        *[dma(2 * slots)] * 4,
        *[dma(hops + 2)] * 2,
        *[dma(6 + extra)] * 12,
    ]
    total = slots * n * rows
    return pl.pallas_call(
        functools.partial(backward_kernel, batch),
        in_specs=anywhere(15) + in_vmem(3),
        out_specs=anywhere(6) + in_vmem(1),
        out_shape=outs,
        scratch_shapes=scratch,
        compiler_params=pltpu.CompilerParams(
            collective_id=2, has_side_effects=True, vmem_limit_bytes=VMEM_LIMIT
        ),
        cost_estimate=pl.CostEstimate(
            flops=total * (20 * feat * width + 40 * width * width),
            transcendentals=total * 6 * width,
            bytes_accessed=2 * total * (6 * feat),
        ),
        name="backward",
    )(tokens, middle, gmid, res, *saved, sums, *q4, wo, gain_one, gain_head, two_part)


def widen_kernel(unit, qk, vg, out, *targets):
    width = qk.shape[2] // 2
    for c, at in enumerate((2, 0, 1)):
        targets[5 + at][...] = unit[c, 0].astype(F32)
    targets[0][...] = qk[0, :, :width].astype(F32)
    targets[1][...] = qk[0, :, width:].astype(F32)
    targets[2][...] = vg[0, :, :width].astype(F32)
    targets[3][...] = vg[0, :, width:].astype(F32)
    targets[4][...] = out[0].astype(F32)


def widen(unit, qk, vg, out):
    eighth, feat = unit.shape[2:]
    width = qk.shape[2] // 2
    block = lambda dims: pl.BlockSpec((1,) + dims, lambda i: (i, 0, 0))
    flat = lambda dims: pl.BlockSpec(dims, lambda i: (i, 0))
    whole = lambda rows, cols: jax.ShapeDtypeStruct((8 * rows, cols), F32)
    return pl.pallas_call(
        widen_kernel,
        grid=(8,),
        in_specs=[
            pl.BlockSpec((3, 1, eighth, feat), lambda i: (0, i, 0, 0)),
            block(qk.shape[1:]),
            block(vg.shape[1:]),
            block(out.shape[1:]),
        ],
        out_specs=[flat((feat // 8, width))] * 4
        + [flat((width // 8, feat))]
        + [flat((eighth, feat))] * 3,
        out_shape=[whole(feat // 8, width)] * 4 + [whole(width // 8, feat)] + [whole(eighth, feat)] * 3,
        compiler_params=pltpu.CompilerParams(vmem_limit_bytes=VMEM_LIMIT),
        name="widen",
    )(unit, qk, vg, out)


def on_device(
    batch,
    tokens,
    lengths,
    assignment,
    query_weight,
    key_weight,
    value_weight,
    gate_weight,
    out_weight,
    up_weight,
    pair_weight,
    down_weight,
    attention_norm_gain,
    mlp_gain,
    head_gain,
    cotangent,
):
    slots = tokens.shape[0]
    width = query_weight.shape[1]
    place = lax.axis_index("seq").astype(jnp.int32)
    seq_ids = lax.broadcasted_iota(jnp.int32, (slots, lengths.shape[0]), 1)
    slot_length = jnp.sum(jnp.where(assignment[:, None] == seq_ids, lengths[None, :], 0), axis=1)
    q4 = (query_weight, key_weight, value_weight, gate_weight)
    gain_one, gain_two, gain_head = attention_norm_gain[None], mlp_gain[None], head_gain[None]
    h_one, qkvg, mixed, gated, states, _, res, middle, gmid, sums, two_part = forward(
        slot_length, tokens, cotangent, q4, out_weight, up_weight.T, pair_weight.T, down_weight,
        gain_one, gain_two, gain_head,
    )
    result, grad_inputs, unit_total, qk_total, vg_total, out_total, gains = backward(
        batch, tokens, middle, gmid, res, (qkvg, mixed, states, h_one, gated), sums, q4, out_weight,
        gain_one, gain_head, two_part,
    )
    grad_qw, grad_kw, grad_vw, grad_gw, grad_outw, grad_upw, grad_pairw, grad_down = widen(
        unit_total, qk_total, vg_total, out_total
    )
    head_total = lax.dynamic_slice(gains[2], (place * width,), (width,))
    return (
        result,
        grad_inputs,
        grad_qw,
        grad_kw,
        grad_vw,
        grad_gw,
        grad_outw,
        grad_upw.T,
        grad_pairw.T,
        grad_down,
        gains[0],
        gains[1],
        head_total,
    )


def solution(mesh):
    return jax.shard_map(
        functools.partial(on_device, mesh.shape["batch"]),
        mesh=mesh,
        in_specs=(
            P("batch", "seq", None),
            P(),
            P("batch"),
            P(None, "seq"),
            P(None, "seq"),
            P(None, "seq"),
            P(None, "seq"),
            P("seq", None),
            P(None, "seq"),
            P(None, "seq"),
            P("seq", None),
            P(),
            P(),
            P("seq"),
            P("batch", "seq", None),
        ),
        out_specs=(
            P("batch", "seq", None),
            P("batch", "seq", None),
            P(None, "seq"),
            P(None, "seq"),
            P(None, "seq"),
            P(None, "seq"),
            P("seq", None),
            P(None, "seq"),
            P(None, "seq"),
            P("seq", None),
            P(),
            P(),
            P("seq"),
        ),
        check_vma=False,
    )
```

time: 1110 us -> 381 us (0.34)
  waiting for transfers between devices: 729 us -> 0 us
  Pallas kernels: 0 us -> 373 us
  matrix products: 209 us -> 0 us
  blocking collectives: 59.7 us -> 0 us
  other arithmetic: 48.2 us -> 1.36 us
  local copies, waits for them, and re-layouts: 42.2 us -> 5.51 us
  between operations: 14.6 us -> 0.69 us
    psum x1 -> x0, waiting for transfers between devices: 437 us -> none  [on_device(): lax.psum((grad_qw, grad_kw, grad_vw, grad_gw, grad_outw, grad_upw, grad_p...]
    pallas_call x0 -> x3, Pallas kernels: none -> 373 us  [the longest x1 186 us: backward(): pl.pallas_call(functools.partial(backward_kernel, batch), in_specs=anywhe...]
    dot_general x30 -> x0, matrix products: 209 us -> none  [the longest x5 48.4 us: weight_grad(): lax.dot_general(inputs, grads, (((0, 1), (0, 1)), ((), ())), preferred_el...]
    all_gather x4 -> x0, waiting for transfers between devices: 175 us -> none  [the longest x1 46.5 us: on_device(): lax.all_gather(grad_middle.astype(jnp.bfloat16), 'seq', axis=0, tiled=True)]
    reduce_scatter x4 -> x0, waiting for transfers between devices: 116 us -> none  [the longest x1 58.3 us: on_device(): lax.psum_scatter((matmul_back(grad_up, up_weight) + matmul_back(grad_pair...]
    psum x2 -> x0, blocking collectives: 59.7 us -> none  [the longest x1 37.4 us: on_device(): lax.psum((gain_one_part, gain_two_part), ('batch', 'seq'))]
    unnamed x134 -> x6, local copies, waits for them, and re-layouts: 26 us -> 4.34 us
    convert_element_type x6 -> x0, other arithmetic: 17.4 us -> none  [the longest x1 5.11 us: on_device(): keys = (jax.nn.softplus(pre_key) * valid[..., None]).astype(jnp.bfloat16)]
  transfers between devices with their start and end apart: 9 -> 0, of which waited for: 7 -> 0; matrix products, arithmetic and copies ran while one was open for 8% -> 0% of each run, Pallas kernels for 0% -> 0%
where the time goes in v1:
time: 381 us
  Pallas kernels  373 us (98%)
  local copies, waits for them, and re-layouts  5.51 us (1%)
    pallas_call x1, Pallas kernels, backward(): pl.pallas_call(functools.partial(backward_kernel, batch), in_specs=anywhe...  186 us
    pallas_call x1, Pallas kernels, forward(): pl.pallas_call(forward_kernel, in_specs=[pl.BlockSpec(memory_space=pltpu....  178 us
    pallas_call x1, Pallas kernels, widen(): pl.pallas_call(widen_kernel, grid=(8,), in_specs=[pl.BlockSpec((3, 1, eig...  8.89 us

profile of v1, /device:TPU:0, one launch (start us, length us, event | category | flops | bytes accessed | tf_op | source)
XLA Modules:
  0.0 380.6 jit_solution(4030953196568672757)
XLA Ops:
  0.6 1.4 select_reduce_fusion.length_ref
  2.0 178.4 %forward.1 = (bf16[3,4,256,1024]{3,2,1,0:T(8,128)(2,1)}, bf16[3,4,4,256,256]{4,3,2,1,0:T(8,128)(2,1)}, bf16[3,4,256,256]{3,2,1,0:T(8,128)(2,1)}, bf16[3,4,256,25...) custom-call(s32[3]{0:T(128)} %select_reduce_fusion.length_ref, ...), custom_call_target="tpu_custom_call" | custom-call | flops 51136954368 | bytes 50724864 | tf_op jit(solution)/shard_map/forward/pallas_call | solution.py:656
  180.4 185.8 %backward.1 = (bf16[3,256,1024]{2,1,0:T(8,128)(2,1)}, f32[3,256,1024]{2,1,0:T(8,128)}, bf16[3,8,88,1024]{3,2,1,0:T(8,128)(2,1)}, bf16[8,128,512]{2,1,0:T(8,128)(...) custom-call(bf16[3,256,1024]{2,1,0:T(8,128)(2,1)} %tokens.3, ...), custom_call_target="tpu_custom_call" | custom-call | flops 24159191040 | bytes 37748736 | tf_op jit(solution)/shard_map/backward/pallas_call | solution.py:1078
  366.1 0.0 copy-start.1
  366.2 8.9 %widen.1 = (f32[1024,256]{1,0:T(8,128)}, f32[1024,256]{1,0:T(8,128)}, f32[1024,256]{1,0:T(8,128)}, f32[1024,256]{1,0:T(8,128)}, f32[256,1024]{1,0:T(8,128)}, /*i...) custom-call(bf16[3,8,88,1024]{3,2,1,0:T(8,128)(2,1)} %get-tuple-element.50.unit, ...), custom_call_target="tpu_custom_call" | custom-call | tf_op jit(solution)/shard_map/widen/pallas_call | solution.py:1113
  375.1 0.0 copy-start
  375.1 0.0 copy-done.1
  375.1 0.6 fusion
  375.7 0.6 constant_dynamic-slice_fusion
  376.2 2.7 copy.30
  378.9 0.0 copy-done
  378.9 1.7 copy.31
Async XLA Ops:
  366.1 8.9 %copy-start.1 = (f32[3,1024]{1,0:T(4,128)S(1)}, f32[3,1024]{1,0:T(4,128)}, u32[]{:S(2)}) copy-start(f32[3,1024]{1,0:T(4,128)} %get-tuple-element.62) | copy-start | bytes 36868
  375.1 3.9 %copy-start = (f32[3,256,1024]{2,1,0:T(8,128)S(1)}, f32[3,256,1024]{2,1,0:T(8,128)}, u32[]{:S(2)}) copy-start(f32[3,256,1024]{2,1,0:T(8,128)} %get-tuple-element.80) | copy-start | bytes 9437188

commit v2 on v1

--- a/solution.py
+++ b/solution.py
@@ -178,7 +178,8 @@
 
 
 class Reduce:
-    def __init__(self, peers, bits, send, work, came, total, sems, local):
+    def __init__(self, peers, bits, send, work, came, total, sems, local, early=None):
+        self.early = early
         self.peers, self.send, self.work, self.came, self.total = peers, send, work, came, total
         self.sems, self.local = sems, local
         self.bits = bits
@@ -225,7 +226,10 @@
         self.stage = max(self.stage, t + 1)
         if t < last:
             _, b1, _ = self.b
-            self.hop(t).wait_recv()
+            if t == 0 and self.early is not None:
+                self.early.wait()
+            else:
+                self.hop(t).wait_recv()
             if t > 2:
                 self.hop(t).wait_send()
             base, first, count = (
@@ -256,7 +260,8 @@
 
     def sent(self):
         for t in range(3):
-            self.hop(t).wait_send()
+            if t or self.early is None:
+                self.hop(t).wait_send()
             self.back(t).wait_send()
 
 
@@ -289,17 +294,19 @@
 
 
 def forward_kernel(
+    batch,
     length_ref, tokens, cotangent, wq, wk, wv, wg, wo, up, pair, down, gain_one, gain_two, gain_head,
     h1_out, qkvg_out, mixed_out, gated_out, state_out, g_out, res_out, middle_out, gmid_out, sums_out,
-    gain_out,
-    tok, w4, wo_v, up_v, pair_v, down_v, h1, h2, part, came, far, middle, gmid, state,
+    down_came, gain_out,
+    tok, w4, wo_v, up_v, pair_v, down_v, h1, h2, part, came, far, middle, state,
     load_sem, save_sem, gload_sem, h1_send, h1_recv, h2_send, h2_recv, g_send, g_recv,
-    a_send, a_recv, b_send, b_recv,
+    a_send, a_recv, b_send, b_recv, y_send, y_recv,
 ):
     slots, rows, feat = tok.shape
     width, hid, wide = wo_v.shape[0], down.shape[0], down_v.shape[0]
     heads = width // HD
-    peers = Peers()
+    peers = Peers(batch)
+    peers.hops = 1
 
     def load(source, target, index):
         return pltpu.make_async_copy(source, target, load_sem.at[index])
@@ -317,6 +324,10 @@
     for one in loads:
         one.start()
     peers.meet()
+    down_hop = remote(
+        sums_out.at[0, pl.ds((1 - peers.bit(0)) * 4, 4)], down_came, (y_send, y_recv), 0,
+        peers.partner(0),
+    )
     first = Gather(peers, h1, (h1_send, h1_recv))
     second = Gather(peers, h2, (h2_send, h2_recv))
     grads = Gather(peers, g_out, (g_send, g_recv), lambda k: cotangent.at[k])
@@ -324,7 +335,7 @@
     scatter_a = Scatter(peers, *buffers, (a_send, a_recv))
     scatter_b = Scatter(peers, *buffers, (b_send, b_recv))
     g1, g2, gh = gain_one[...], gain_two[...], gain_head[...]
-
+    grads.chip_hop(0).start()
     loads[0].wait()
 
     def norm_first(k):
@@ -360,7 +371,7 @@
             @pl.when(k == 1)
             def _():
                 scatter_a.middle_step(0)
-                grads.chip_hop(0).start()
+                grads.chip_hop(1).start()
 
             @pl.when(k > 0)
             def _():
@@ -437,12 +448,9 @@
         second.start(k)
         scatter_a.sent(k)
 
-    def follow(k):
+    finish_attend(0)
+    for k in range(1, slots):
         scatter_a.middle_step(k)
-        grads.chip_hop(k).start()
-
-    finish_attend(0)
-    follow(1)
     h1_save = pltpu.make_async_copy(h1, h1_out, save_sem.at[4])
     h1_save.start()
     for one in loads[6:]:
@@ -459,30 +467,41 @@
 
         loop(9, clear)
 
+        def gload(k, j):
+            return pltpu.make_async_copy(g_out.at[k, j], gbuf.at[j], gload_sem.at[j])
+
+        tile = wide // 3
+        eighth = hid // 8
+
+        def weigh(c, left, right):
+            def one(m):
+                cols = pl.ds(pl.multiple_of(m * tile, tile), tile)
+                sums[c, cols] += tn(left[:, :, cols].reshape(BLOCKS * rows, tile), right())
+
+            loop(3, one)
+
+        def sums_save(c):
+            return pltpu.make_async_copy(staged, sums_out.at[c], save_sem.at[6])
+
+        def settle_sums(c):
+            def convert(p):
+                staged[p] = sums[c, pl.ds(pl.multiple_of(p * eighth, 8), eighth)].astype(BF)
+
+            loop(8, convert)
+            sums_save(c).start()
+
         def unit(k):
-            second.forward(k)
-            grads.forward(k)
+            second.core_hop(k).wait_recv()
+            grads.core_hop(k).wait_recv()
+            gload(k, 0).start()
+            gload(k, 1).start()
 
             @pl.when(k > 0)
             def _():
                 unit_save(k - 1).wait()
 
-            second.arrived(k)
-            grads.arrived(k)
-            for j in range(BLOCKS):
-                pltpu.make_async_copy(g_out.at[k, j], gbuf.at[j], gload_sem.at[j]).start()
-
-            def one(t):
-                @pl.when((t == 2) & (k + 1 < slots))
-                def _():
-                    finish_attend(k + 1)
-
-                @pl.when((t == 2) & (k + 2 < slots))
-                def _():
-                    follow(k + 2)
-
-                j = t + (t // 2) * (1 - 2 * (t % 2))
-                pltpu.make_async_copy(g_out.at[k, j], gbuf.at[j], gload_sem.at[j]).wait()
+            def one(j):
+                gload(k, j).wait()
                 hidden, grad = h2[k, j], gbuf[j]
                 up_part = nt(hidden, up_v[...])
                 pair_part = nt(hidden, pair_v[...])
@@ -496,12 +515,35 @@
                 gp_s[j] = grad_pair
                 part[k, spot(j)] = (nn(grad_up, up_v[...]) + nn(grad_pair, pair_v[...])).astype(BF)
 
-                @pl.when(t == 2)
+            def block(j):
+                @pl.when((j == 2) & (k == 1))
                 def _():
-                    scatter_b.start(k)
-
-            loop(BLOCKS, one)
+                    finish_attend(2)
+                    grads.chip_hop(2).start()
+
+                @pl.when(j == 2)
+                def _():
+                    second.forward(k)
+                    grads.forward(k)
+                    gload(k, 2).start()
+
+                @pl.when(j == 3)
+                def _():
+                    second.passed_on(k).wait_recv()
+                    grads.passed_on(k).wait_recv()
+                    gload(k, 3).start()
+
+                one(j)
+
+            loop(BLOCKS, block)
             unit_save(k).start()
+            scatter_b.start(k)
+            hidden_all = lambda: h2[k].reshape(BLOCKS * rows, feat)
+            weigh(0, prod_s, lambda: gbuf[...].reshape(BLOCKS * rows, feat))
+
+            @pl.when(k == 0)
+            def _():
+                finish_attend(1)
 
             @pl.when(k == 1)
             def _():
@@ -511,37 +553,23 @@
             def _():
                 scatter_b.middle_step(k)
 
-            hidden_all = h2[k].reshape(BLOCKS * rows, feat)
-            grad_all = gbuf[...].reshape(BLOCKS * rows, feat)
-            tile = wide // 3
-
-            def weigh(m):
-                cols = pl.ds(pl.multiple_of(m * tile, tile), tile)
-
-                def of(ref):
-                    return ref[:, :, cols].reshape(BLOCKS * rows, tile)
-
-                sums[0, cols] += tn(of(prod_s), grad_all)
-                sums[1, cols] += tn(of(gu_s), hidden_all)
-                sums[2, cols] += tn(of(gp_s), hidden_all)
-
-            loop(3, weigh)
+            @pl.when(k == slots - 1)
+            def _():
+                settle_sums(0)
+
+            weigh(1, gu_s, hidden_all)
+
+            @pl.when(k == slots - 1)
+            def _():
+                sums_save(0).wait()
+                down_hop.start()
+                settle_sums(1)
+
+            weigh(2, gp_s, hidden_all)
 
         loop(slots, unit)
-        eighth = hid // 8
-
-        def sums_save(c):
-            return pltpu.make_async_copy(staged, sums_out.at[c], save_sem.at[6])
-
-        for c in range(3):
-            if c:
-                sums_save(c - 1).wait()
-
-            def convert(p):
-                staged[p] = sums[c, pl.ds(pl.multiple_of(p * eighth, 8), eighth)].astype(BF)
-
-            loop(8, convert)
-            sums_save(c).start()
+        sums_save(1).wait()
+        settle_sums(2)
         sums_save(2).wait()
         unit_save(slots - 1).wait()
 
@@ -562,30 +590,29 @@
     own_grads.wait()
     gain_out[...] = jnp.zeros_like(gain_out)
 
-    def gmid_save(k):
-        return pltpu.make_async_copy(gmid.at[k % 2], gmid_out.at[k], save_sem.at[11 + k % 2])
-
-    def finish_unit(k):
-        scatter_b.arrived(k)
-
-        @pl.when(k > 1)
-        def _():
-            gmid_save(k - 2).wait()
-
-        def some(r):
-            grad = (
-                part[k, 0, r].astype(F32) + came[k, 0, r].astype(F32) + far[k, r].astype(F32)
-            )
-            normed, scale, _ = normalize(middle[k, r], g2)
-            gain_out[...] += jnp.sum(grad * normed, axis=0, keepdims=True)
-            gmid[k % 2, r] = tok[k, r].astype(F32) + norm_back(grad, normed, scale, g2)
-
-        by_rows(rows, some)
-        gmid_save(k).start()
-
-    loop(slots, finish_unit)
-    for k in range(max(slots - 2, 0), slots):
-        gmid_save(k).wait()
+    def finish_all(gmid):
+        def gmid_save(k):
+            return pltpu.make_async_copy(gmid.at[k], gmid_out.at[k], save_sem.at[10 + k])
+
+        def finish_unit(k):
+            scatter_b.arrived(k)
+
+            def some(r):
+                grad = (
+                    part[k, 0, r].astype(F32) + came[k, 0, r].astype(F32) + far[k, r].astype(F32)
+                )
+                normed, scale, _ = normalize(middle[k, r], g2)
+                gain_out[...] += jnp.sum(grad * normed, axis=0, keepdims=True)
+                gmid[k, r] = tok[k, r].astype(F32) + norm_back(grad, normed, scale, g2)
+
+            by_rows(rows, some)
+            gmid_save(k).start()
+
+        loop(slots, finish_unit)
+        for k in range(slots):
+            gmid_save(k).wait()
+
+    pl.run_scoped(finish_all, v((slots, rows, feat), F32))
     for save in (h1_save, middle_save):
         save.wait()
 
@@ -596,6 +623,7 @@
         scatter_b.sent(k)
 
     loop(slots, settle)
+    down_hop.wait()
 
 
 def dma(n):
@@ -610,7 +638,7 @@
     return [pl.BlockSpec(memory_space=pltpu.VMEM)] * n
 
 
-def forward(lengths, tokens, cotangent, q4, wo, up, pair, down, gain_one, gain_two, gain_head):
+def forward(batch, lengths, tokens, cotangent, q4, wo, up, pair, down, gain_one, gain_two, gain_head):
     slots, rows, feat = tokens.shape
     width, hid = wo.shape[0], down.shape[0]
     n = BLOCKS
@@ -628,6 +656,7 @@
         shape((slots, rows, feat), F32),
         shape((slots, rows, feat), F32),
         shape((3, 8, hid // 8, feat), BF),
+        shape((4, hid // 8, feat), BF),
         shape((1, feat), F32),
     ]
     v = pltpu.VMEM
@@ -644,19 +673,19 @@
         v((slots, 2, rows, feat), BF),
         v((slots, rows, feat), BF),
         v((slots, rows, feat), F32),
-        v((2, rows, feat), F32),
         v((width, width), F32),
         dma(10),
         dma(13),
         dma(n),
         *[dma(3 * slots)] * 6,
         *[dma(2 * slots)] * 4,
+        *[dma(1)] * 2,
     ]
     total = slots * n * rows
     return pl.pallas_call(
-        forward_kernel,
+        functools.partial(forward_kernel, batch),
         in_specs=[pl.BlockSpec(memory_space=pltpu.SMEM)] + anywhere(10) + in_vmem(3),
-        out_specs=anywhere(10) + in_vmem(1),
+        out_specs=anywhere(11) + in_vmem(1),
         out_shape=outs,
         scratch_shapes=scratch,
         compiler_params=pltpu.CompilerParams(
@@ -673,7 +702,7 @@
 
 def backward_kernel(
     batch,
-    tokens, middle, gmid, res, qkvg_in, mixed_in, state_in, h1_in, gated_in, sums_in,
+    tokens, middle, gmid, res, qkvg_in, mixed_in, state_in, h1_in, gated_in, sums_in, down_came,
     wq, wk, wv, wg, wo, gain_one, gain_head, two_part,
     result, grad_tokens, unit_total, qk_total, vg_total, out_total, gains,
     w4, wo_v, gm, part, came, far, res_mid, came2, far2, state,
@@ -701,7 +730,8 @@
         pltpu.make_async_copy(sums_in.at[c, pl.ds(half * 4, 4)], unit_work.at[c], unit_sem.at[c])
         for c in range(3)
     ]
-    for one in (*weight_loads, *unit_loads):
+    early = pltpu.make_async_copy(down_came, unit_came.at[0, pl.ds(0, 4)], unit_sem.at[3])
+    for one in (*weight_loads, *unit_loads, early):
         one.start()
     gather = Gather(peers, gm, (gm_send, gm_recv))
     scatter = Scatter(
@@ -713,7 +743,7 @@
     unit_sums = [
         Reduce(
             peers, (0, 1, 2), sums_in.at[c, pl.ds((1 - half) * 4, 4)], unit_work.at[c],
-            unit_came.at[c], unit_total.at[c], sems, local_sem.at[c],
+            unit_came.at[c], unit_total.at[c], sems, local_sem.at[c], None if c else early,
         )
         for c, sems in enumerate(((d_send, d_recv), (u_send, u_recv), (p_send, p_recv)))
     ]
@@ -732,8 +762,8 @@
     gains[...] = jnp.zeros_like(gains)
     gains[1:2] = two_part[...]
     peers.meet()
-    for one in unit_sums:
-        one.begin()
+    pair_sum.begin()
+    up_sum.begin()
     v = pltpu.VMEM
 
     def begin_all(gmv):
@@ -756,6 +786,7 @@
         one.wait()
     for one in unit_loads:
         one.wait()
+    down_sum.step(0)
     block = same_head(width)
     ones = block.astype(BF)
 
@@ -773,8 +804,32 @@
         for one in slot_loads(0):
             one.start()
 
+        plan = {
+            (0, -1): ((down_sum, 1),),
+            (0, 1): ((pair_sum, 0),),
+            (0, 3): ((down_sum, 2),),
+            (0, 4): ((pair_sum, 1),),
+            (1, -1): ((up_sum, 0), (down_sum, 3)),
+            (1, 2): ((pair_sum, 2),),
+            (1, 3): ((up_sum, 1),),
+            (1, 7): ((down_sum, 4),),
+            (2, -1): ((pair_sum, 3),),
+            (2, 2): ((up_sum, 2),),
+        }
+
+        def hooks(k, point):
+            for (slot, where), actions in plan.items():
+                if isinstance(point, int) and point != where:
+                    continue
+
+                @pl.when((k == slot) & (point == where))
+                def _():
+                    for one, stage in actions:
+                        one.step(stage)
+
         def attend_back(k):
             b = k % 2
+            hooks(k, -1)
             gather.forward(k)
 
             @pl.when(k > 0)
@@ -792,21 +847,7 @@
             state[...] = jnp.zeros_like(state)
 
             def chunk(step):
-                @pl.when((k == 0) & (step == 2))
-                def _():
-                    down_sum.step(0)
-
-                @pl.when((k == 1) & (step == 1))
-                def _():
-                    down_sum.step(2)
-                    up_sum.step(1)
-
-                @pl.when((k == 2) & (step == 1))
-                def _():
-                    down_sum.step(4)
-                    up_sum.step(3)
-                    pair_sum.step(1)
-
+                hooks(k, step)
                 i = BLOCKS - 1 - step
                 j = peers.relative(i)
                 grad_gated = nt(gm[k, j], wo_v[...]).astype(BF).astype(F32)
@@ -850,20 +891,10 @@
             scatter.start(k)
             results.middle_step(k)
 
-            @pl.when(k == 0)
-            def _():
-                down_sum.step(1)
-                up_sum.step(0)
-
-            @pl.when(k == 1)
-            def _():
-                down_sum.step(3)
-                up_sum.step(2)
-                pair_sum.step(0)
-
             pre_all = pre[...].reshape(BLOCKS * rows, 4 * width)
 
             def weigh(m):
+                hooks(k, BLOCKS + m)
                 cols = pl.ds(pl.multiple_of(m * 256, 256), 256)
                 term = tn(h1[b, :, :, cols].reshape(BLOCKS * rows, 256), pre_all)
                 sums[cols] = jnp.where(k > 0, sums[cols], 0.0) + term
@@ -891,7 +922,7 @@
             out_send[q] = out_acc[small(1 - half)].astype(BF)
 
         loop(4, fill_all)
-        for one in (vg_sum, out_sum, qk_sum):
+        for one in (out_sum, vg_sum, qk_sum):
             one.begin()
 
     pl.run_scoped(
@@ -920,7 +951,7 @@
             return pltpu.make_async_copy(gmv.at[k], grad_tokens.at[k], save_sem.at[k])
 
         def result_save(k):
-            return pltpu.make_async_copy(tok.at[k], result.at[k], save_sem.at[slots + k])
+            return pltpu.make_async_copy(kept.at[k], result.at[k], save_sem.at[slots + k])
 
         def finish(k):
             scatter.arrived(k)
@@ -946,60 +977,47 @@
                     + came2[k, 0, r].astype(F32)
                     + far2[k, r].astype(F32)
                 )
-                tok[k, r] = total.astype(BF)
+                kept[k, r] = total.astype(BF)
 
             by_rows(rows, some)
             result_save(k).start()
 
-        up_sum.step()
-        pair_sum.step()
         for one in finals:
             one.wait()
-        finish(0)
-        finish_result(0)
-        qk_sum.step()
-        pair_sum.step()
-        vg_sum.step()
-        out_sum.step()
-        finish(1)
-        finish_result(1)
-        qk_sum.step()
-        pair_sum.step()
-        vg_sum.step()
-        out_sum.step()
-        up_sum.step()
-        qk_sum.step()
-        for k in range(2, slots):
-            finish(k)
-            finish_result(k)
-        lane = lax.broadcasted_iota(jnp.int32, (1, BLOCKS * width), 1) // width
-        spread = jnp.concatenate([head_part[...]] * BLOCKS, axis=1)
-        gains[2:3] = jnp.where(lane == peers.place, spread, 0.0)
         others = [peers.beside, peers.across] + [peers.partner(h) for h in range(peers.hops)]
 
         def gain_hop(t):
             return remote(gains, gain_came.at[t], (gain_send, gain_recv), t, others[t])
 
-        def gain_step(t):
+        def gain_begin():
+            lane = lax.broadcasted_iota(jnp.int32, (1, BLOCKS * width), 1) // width
+            spread = jnp.concatenate([head_part[...]] * BLOCKS, axis=1)
+            gains[2:3] = jnp.where(lane == peers.place, spread, 0.0)
+            gain_hop(0).start()
+
+        hop = iter(range(len(others)))
+
+        def gain_step():
+            t = next(hop, None)
+            if t is None:
+                return
             gain_hop(t).wait_recv()
             gain_hop(t).wait_send()
             gains[...] += gain_came[t]
             if t + 1 < len(others):
                 gain_hop(t + 1).start()
 
-        gain_hop(0).start()
-        waiting = [vg_sum, out_sum, pair_sum, qk_sum, up_sum]
-        order = [one for _ in range(8) for one in waiting]
-        hop = 0
-        for one in order:
-            if one.stage < one.steps():
-                one.step()
-                if hop < len(others):
-                    gain_step(hop)
-                    hop += 1
-        while hop < len(others):
-            gain_step(hop)
-            hop += 1
+        o, v, q = out_sum.step, vg_sum.step, qk_sum.step
+        u, p = up_sum.step, pair_sum.step
+        for one in (
+            (finish, 0), (finish_result, 0), (finish_result, 1), (o,), (finish, 1), (q,), (p,), (o,),
+            (v,), (finish_result, 2), (q,), (u,), (v,), (o,), (finish, 2), (gain_begin,), (q,),
+            (gain_step,), (u,), (v,), (gain_step,), (o,), (q,), (gain_step,), (v,), (o,),
+            (gain_step,), (v,), (gain_step,), (q,),
+        ):
+            one[0](*one[1:])
+        for _ in others:
+            gain_step()
         for one in (*unit_sums, qk_sum, vg_sum, out_sum):
             while one.stage < one.steps():
                 one.step()
@@ -1024,7 +1042,7 @@
     )
 
 
-def backward(batch, tokens, middle, gmid, res, saved, sums, q4, wo, gain_one, gain_head, two_part):
+def backward(batch, tokens, middle, gmid, res, saved, sums, down_came, q4, wo, gain_one, gain_head, two_part):
     slots, rows, feat = tokens.shape
     width = wo.shape[0]
     eighth = sums.shape[2]
@@ -1067,7 +1085,7 @@
         dma(7),
         dma(10),
         dma(2 * slots),
-        dma(3),
+        dma(4),
         dma(6),
         *[dma(3 * slots)] * 2,
         *[dma(2 * slots)] * 4,
@@ -1077,7 +1095,7 @@
     total = slots * n * rows
     return pl.pallas_call(
         functools.partial(backward_kernel, batch),
-        in_specs=anywhere(15) + in_vmem(3),
+        in_specs=anywhere(16) + in_vmem(3),
         out_specs=anywhere(6) + in_vmem(1),
         out_shape=outs,
         scratch_shapes=scratch,
@@ -1090,7 +1108,7 @@
             bytes_accessed=2 * total * (6 * feat),
         ),
         name="backward",
-    )(tokens, middle, gmid, res, *saved, sums, *q4, wo, gain_one, gain_head, two_part)
+    )(tokens, middle, gmid, res, *saved, sums, down_came, *q4, wo, gain_one, gain_head, two_part)
 
 
 def widen_kernel(unit, qk, vg, out, *targets):
@@ -1153,12 +1171,13 @@
     slot_length = jnp.sum(jnp.where(assignment[:, None] == seq_ids, lengths[None, :], 0), axis=1)
     q4 = (query_weight, key_weight, value_weight, gate_weight)
     gain_one, gain_two, gain_head = attention_norm_gain[None], mlp_gain[None], head_gain[None]
-    h_one, qkvg, mixed, gated, states, _, res, middle, gmid, sums, two_part = forward(
-        slot_length, tokens, cotangent, q4, out_weight, up_weight.T, pair_weight.T, down_weight,
+    h_one, qkvg, mixed, gated, states, _, res, middle, gmid, sums, down_came, two_part = forward(
+        batch, slot_length, tokens, cotangent, q4, out_weight, up_weight.T, pair_weight.T, down_weight,
         gain_one, gain_two, gain_head,
     )
     result, grad_inputs, unit_total, qk_total, vg_total, out_total, gains = backward(
-        batch, tokens, middle, gmid, res, (qkvg, mixed, states, h_one, gated), sums, q4, out_weight,
+        batch, tokens, middle, gmid, res, (qkvg, mixed, states, h_one, gated), sums, down_came, q4,
+        out_weight,
         gain_one, gain_head, two_part,
     )
     grad_qw, grad_kw, grad_vw, grad_gw, grad_outw, grad_upw, grad_pairw, grad_down = widen(

time: 381 us -> 359 us (0.942)
  Pallas kernels: 373 us -> 351 us
    pallas_call x1, Pallas kernels: 186 us -> 164 us  [backward(): pl.pallas_call(functools.partial(backward_kernel, batch), in_specs=anywhe...]
where the time goes in v2:
time: 359 us; the launch traced here: 358 us
  Pallas kernels  351 us (98%)
  local copies, waits for them, and re-layouts  5.51 us (2%)
    pallas_call x1, Pallas kernels, forward(): pl.pallas_call(functools.partial(forward_kernel, batch), in_specs=[pl.Blo...  178 us
    pallas_call x1, Pallas kernels, backward(): pl.pallas_call(functools.partial(backward_kernel, batch), in_specs=anywhe...  164 us
    pallas_call x1, Pallas kernels, widen(): pl.pallas_call(widen_kernel, grid=(8,), in_specs=[pl.BlockSpec((3, 1, eig...  8.89 us

profile of v2, /device:TPU:0, one launch (start us, length us, event | category | flops | bytes accessed | tf_op | source)
XLA Modules:
  0.0 358.1 jit_solution(7840353655239666508)
XLA Ops:
  0.6 1.4 select_reduce_fusion.length_ref
  2.0 178.0 %forward.1 = (bf16[3,4,256,1024]{3,2,1,0:T(8,128)(2,1)}, bf16[3,4,4,256,256]{4,3,2,1,0:T(8,128)(2,1)}, bf16[3,4,256,256]{3,2,1,0:T(8,128)(2,1)}, bf16[3,4,256,25...) custom-call(s32[3]{0:T(128)} %select_reduce_fusion.length_ref, ...), custom_call_target="tpu_custom_call" | custom-call | flops 51136954368 | bytes 50724864 | tf_op jit(solution)/shard_map/forward/pallas_call | solution.py:685
  180.0 163.7 %backward.1 = (bf16[3,256,1024]{2,1,0:T(8,128)(2,1)}, f32[3,256,1024]{2,1,0:T(8,128)}, bf16[3,8,88,1024]{3,2,1,0:T(8,128)(2,1)}, bf16[8,128,512]{2,1,0:T(8,128)(...) custom-call(bf16[3,256,1024]{2,1,0:T(8,128)(2,1)} %tokens.3, ...), custom_call_target="tpu_custom_call" | custom-call | flops 24159191040 | bytes 37748736 | tf_op jit(solution)/shard_map/backward/pallas_call | solution.py:1096
  343.7 0.0 copy-start.1
  343.7 8.9 %widen.1 = (f32[1024,256]{1,0:T(8,128)}, f32[1024,256]{1,0:T(8,128)}, f32[1024,256]{1,0:T(8,128)}, f32[1024,256]{1,0:T(8,128)}, f32[256,1024]{1,0:T(8,128)}, /*i...) custom-call(bf16[3,8,88,1024]{3,2,1,0:T(8,128)(2,1)} %get-tuple-element.52.unit, ...), custom_call_target="tpu_custom_call" | custom-call | tf_op jit(solution)/shard_map/widen/pallas_call | solution.py:1131
  352.6 0.0 copy-start
  352.6 0.0 copy-done.1
  352.6 0.6 fusion
  353.2 0.6 constant_dynamic-slice_fusion
  353.8 2.7 copy.30
  356.4 0.0 copy-done
  356.4 1.7 copy.31
Async XLA Ops:
  343.7 8.9 %copy-start.1 = (f32[3,1024]{1,0:T(4,128)S(1)}, f32[3,1024]{1,0:T(4,128)}, u32[]{:S(2)}) copy-start(f32[3,1024]{1,0:T(4,128)} %get-tuple-element.64) | copy-start | bytes 36868
  352.6 3.9 %copy-start = (f32[3,256,1024]{2,1,0:T(8,128)S(1)}, f32[3,256,1024]{2,1,0:T(8,128)}, u32[]{:S(2)}) copy-start(f32[3,256,1024]{2,1,0:T(8,128)} %get-tuple-element.82) | copy-start | bytes 9437188

commit v3 on v0

v3 whole, which is shorter than its diff:
```python
import functools

import jax
import jax.numpy as jnp
from jax import lax
from jax.experimental import pallas as pl
from jax.experimental.pallas import tpu as pltpu
from jax.sharding import PartitionSpec as P

HD = 64
EPS = 1e-05
BF = jnp.bfloat16
F32 = jnp.float32
VMEM_LIMIT = 62 * 1024 * 1024
MESH = pl.DeviceIdType.MESH
BLOCKS = 4


def nn(a, b):
    return lax.dot_general(a, b, (((1,), (0,)), ((), ())), preferred_element_type=F32)


def nt(a, b):
    return lax.dot_general(a, b, (((1,), (1,)), ((), ())), preferred_element_type=F32)


def tn(a, b):
    return lax.dot_general(a, b, (((0,), (0,)), ((), ())), preferred_element_type=F32)


def same_head(width):
    rows = lax.broadcasted_iota(jnp.int32, (width, width), 0) // HD
    cols = lax.broadcasted_iota(jnp.int32, (width, width), 1) // HD
    return rows == cols


def by_head(array):
    rows, width = array.shape
    lane = lax.broadcasted_iota(jnp.int32, (rows, width), 1) // HD
    zero = jnp.zeros_like(array)
    return jnp.concatenate([jnp.where(lane == h, array, zero) for h in range(width // HD)], axis=0)


def causal(rows, heads, transposed):
    one = lax.broadcasted_iota(jnp.int32, (rows, rows), 0)
    two = lax.broadcasted_iota(jnp.int32, (rows, rows), 1)
    keep = (two >= one) if transposed else (one >= two)
    return jnp.concatenate([keep] * heads, axis=1)


def masked(scores, keep):
    return jnp.where(keep, scores, 0.0).astype(BF)


def head_mean(array, ones):
    return nn(array.astype(BF), ones) * (1.0 / HD)


def softplus(v):
    return jnp.maximum(v, 0.0) + jnp.log1p(jnp.exp(-jnp.abs(v)))


def sigmoid_of_softplus(q):
    series = q * (1.0 - q * (0.5 - q * (1.0 / 6.0)))
    return jnp.where(q < 0.03, series, 1.0 - jnp.exp(-q))


def sigmoid(v):
    return 1.0 / (1.0 + jnp.exp(-v))


class Peers:
    def __init__(self, batch=1):
        self.place = lax.axis_index("seq")
        self.group = lax.axis_index("batch")
        self.chip, self.core = self.place // 2, self.place % 2
        self.across = (self.group, (1 - self.chip) * 2 + self.core)
        self.beside = (self.group, self.chip * 2 + 1 - self.core)
        self.hops = batch.bit_length() - 1

    def bit(self, h):
        return (self.group // 2**h) % 2

    def partner(self, h):
        return (self.group + (1 - 2 * self.bit(h)) * 2**h, self.place)

    def meet(self):
        others = [self.across, self.beside] + [self.partner(h) for h in range(self.hops)]
        barrier = pltpu.get_barrier_semaphore()
        for peer in others:
            pl.semaphore_signal(barrier, inc=1, device_id=peer, device_id_type=MESH)
        pl.semaphore_wait(barrier, len(others))

    def relative(self, index):
        return ((index // 2 + self.chip) % 2) * 2 + (index % 2 + self.core) % 2


def spot(j):
    return (j % 2) * 2 + j // 2


def remote(source, target, sems, index, peer):
    send, recv = sems
    return pltpu.make_async_remote_copy(
        src_ref=source,
        dst_ref=target,
        send_sem=send.at[index],
        recv_sem=recv.at[index],
        device_id=peer,
        device_id_type=MESH,
    )


class Gather:
    def __init__(self, peers, buffer, sems, own=None):
        self.peers, self.buffer, self.sems = peers, buffer, sems
        self.own = own or (lambda k: buffer.at[k, 0])

    def chip_hop(self, k):
        return remote(self.own(k), self.buffer.at[k, 2], self.sems, 3 * k, self.peers.across)

    def core_hop(self, k):
        return remote(self.own(k), self.buffer.at[k, 1], self.sems, 3 * k + 1, self.peers.beside)

    def passed_on(self, k):
        return remote(
            self.buffer.at[k, 2], self.buffer.at[k, 3], self.sems, 3 * k + 2, self.peers.beside
        )

    def start(self, k):
        self.chip_hop(k).start()
        self.core_hop(k).start()

    def forward(self, k):
        self.chip_hop(k).wait_recv()
        self.passed_on(k).start()

    def arrived(self, k):
        self.core_hop(k).wait_recv()
        self.passed_on(k).wait_recv()

    def sent(self, k):
        self.chip_hop(k).wait_send()
        self.core_hop(k).wait_send()
        self.passed_on(k).wait_send()


class Scatter:
    def __init__(self, peers, pair, middle, came, far, sems):
        self.peers, self.pair, self.middle = peers, pair, middle
        self.came, self.far, self.sems = came, far, sems

    def core_hop(self, k):
        return remote(self.pair(k), self.came.at[k], self.sems, 2 * k, self.peers.beside)

    def chip_hop(self, k):
        return remote(self.middle(k), self.far.at[k], self.sems, 2 * k + 1, self.peers.across)

    def start(self, k):
        self.core_hop(k).start()

    def middle_step(self, k):
        self.core_hop(k).wait_recv()
        middle = self.middle(k)

        def add(rows):
            middle[rows] = (middle[rows].astype(F32) + self.came[k, 1, rows].astype(F32)).astype(BF)

        by_rows(middle.shape[0], add)
        self.chip_hop(k).start()

    def arrived(self, k):
        self.chip_hop(k).wait_recv()

    def sent(self, k):
        self.core_hop(k).wait_send()
        self.chip_hop(k).wait_send()


class Chain:
    def __init__(self, peers, bits, work, came, room, total, sems, load, source=None, far=None, across=None):
        self.peers, self.sems, self.stages, self.waited = peers, sems, [], set()
        b0, b1, b2 = (peers.bit(h) for h in bits)
        pair = 2 if across == "last" else 1
        start = 0 if pair == 2 else b0 * 4
        kept = (start + b1 * 2 + b2) * pair
        self.kept = kept
        piece = b0 * 4 + b1 * 2 + b2

        def fetch(ref):
            copy = pltpu.make_async_copy(ref, room.at[pl.ds(0, ref.shape[0])], load)
            copy.start()
            copy.wait()

        def add(at, base, count):
            def finish():
                fetch(came.at[pl.ds(at, count)])

                def one(q):
                    work[base + q] = (work[base + q].astype(F32) + room[q].astype(F32)).astype(BF)

                loop(count, one)

            return finish

        def spread():
            fetch(far)

            def one(q):
                work[q] = (work[q].astype(F32) + room[q].astype(F32)).astype(BF)

            loop(8, one)

        def meet():
            fetch(far.at[pl.ds(0, 1)])
            work[kept] = (work[kept].astype(F32) + room[0].astype(F32)).astype(BF)

        def other(base, bit, count):
            return work.at[pl.ds((base + (1 - bit) * count) * pair, count * pair)]

        if across == "first":
            self.stages.append((source.at[pl.ds(8, 8)], far, peers.across, spread))
        first = source.at[pl.ds((1 - b0) * 8, 8)] if pair == 2 else other(0, b0, 4)
        at = 0
        for bit, base, count, h in (
            (b0, start, 4, bits[0]), (b1, start, 2, bits[1]), (b2, start + b1 * 2, 1, bits[2])
        ):
            here = base + (bit * count if count < 4 else 0)
            ref = first if count == 4 else other(base, bit, count)
            self.stages.append(
                (ref, came.at[pl.ds(at, count * pair)], peers.partner(h), add(at, here * pair, count * pair))
            )
            at += count * pair
        for h in range(peers.hops):
            if h not in bits:
                ref = work.at[pl.ds(kept, pair)]
                self.stages.append((ref, came.at[pl.ds(at, pair)], peers.partner(h), add(at, kept, pair)))
                self.waited.add(len(self.stages) - 1)
                at += pair
        if across == "last":
            self.stages.append((work.at[pl.ds(kept + 1, 1)], far.at[pl.ds(0, 1)], peers.across, meet))
        self.local = lambda: pltpu.make_async_copy(
            work.at[pl.ds(kept, 1)], total.at[pl.ds(piece, 1)], load
        )
        for where, h in (
            (pl.ds(piece, 1), bits[2]),
            (pl.ds(b0 * 4 + b1 * 2, 2), bits[1]),
            (pl.ds(b0 * 4, 4), bits[0]),
        ):
            ref = work.at[pl.ds(kept, 1)] if h == bits[2] else total.at[where]
            self.stages.append((ref, total.at[where], peers.partner(h), lambda: None))
        self.count = len(self.stages)

    def hop(self, t):
        source, target, peer, _ = self.stages[t]
        return remote(source, target, self.sems, t, peer)

    def begin(self):
        self.hop(0).start()

    def step(self, t):
        self.hop(t).wait_recv()
        if t in self.waited:
            self.hop(t).wait_send()
        self.stages[t][3]()
        if t == self.count - 4:
            own = self.local()
            own.start()
            own.wait()
        if t + 1 < self.count:
            self.hop(t + 1).start()

    def sent(self):
        for t in range(self.count):
            if t not in self.waited:
                self.hop(t).wait_send()


def by_rows(rows, fn, step=64):
    def one(r, carry):
        fn(pl.ds(pl.multiple_of(r * step, step), step))
        return carry

    lax.fori_loop(0, rows // step, one, 0)


def loop(count, fn):
    def one(k, carry):
        fn(k)
        return carry

    lax.fori_loop(0, count, one, 0)


def normalize(values, gain):
    scale = lax.rsqrt(jnp.mean(values * values, axis=-1, keepdims=True) + EPS)
    normed = values * scale
    return normed, scale, (normed * gain).astype(BF)


def norm_back(grad_out, normed, scale, gain):
    grad_normed = grad_out * gain
    inner = jnp.mean(grad_normed * normed, axis=-1, keepdims=True)
    return scale * (grad_normed - normed * inner)


def block_kernel(
    batch,
    length_ref, tokens, cotangent, wq, wk, wv, wg, wo, up, pair, down, gain_one, gain_two, gain_head,
    result, grad_tokens, unit_total, qk_total, vg_total, out_total, gains,
    qkvg_hbm, mixed_hbm, gated_hbm, state_hbm, gm, other, sums, unit_came, unit_far, qk_came, vg_came,
    out_came,
    tok, w4, wo_v, h1, h2, g, part, came, far, middle, state, gain_came, head_part,
    load_sem, save_sem, slot_sem, mat_sem, chain_sem,
    h1_send, h1_recv, gm_send, gm_recv, h2_send, h2_recv, g_send, g_recv, w_send, w_recv,
    a_send, a_recv, b_send, b_recv, c_send, c_recv, gain_send, gain_recv,
    d_send, d_recv, u_send, u_recv, p_send, p_recv,
    d2_send, d2_recv, u2_send, u2_recv, p2_send, p2_recv, q_send, q_recv, v_send, v_recv, o_send, o_recv,
):
    slots, rows, feat = tok.shape
    width, hid = wo_v.shape[0], down.shape[0]
    heads, eighth = width // HD, feat // 8
    both = 2 * hid
    peers = Peers(batch)
    v = pltpu.VMEM

    def load(source, target, index):
        return pltpu.make_async_copy(source, target, load_sem.at[index])

    loads = [
        load(tokens, tok, 0),
        *(load(w, w4.at[m], 1 + m) for m, w in enumerate((wq, wk, wv, wg))),
        load(wo, wo_v, 5),
        load(cotangent, g.at[:, 0], 6),
    ]
    for one in loads:
        one.start()
    peers.meet()

    mats = (up, pair, down)
    b0, b1, b2 = (peers.bit(h) for h in range(3))

    def columns(first, count):
        return pl.ds(pl.multiple_of(first * eighth, eighth), count * eighth)

    def weight_hop(t, c):
        mine = other.at[c]
        cols = (
            columns(b0 * 4 + b1 * 2 + b2, 1), columns(b0 * 4 + b1 * 2 + b2, 1),
            columns(b0 * 4 + b1 * 2, 2), columns(b0 * 4, 4),
        )[t]
        source = (mats[c] if t == 0 else mine).at[:, cols]
        peer = peers.across if t == 0 else peers.partner(3 - t)
        return remote(source, mine.at[:, cols], (w_send, w_recv), 4 * c + t, peer)

    def weight_step(t, c):
        weight_hop(t - 1, c).wait_recv()
        if t < 4:
            weight_hop(t, c).start()

    for c in range(3):
        weight_hop(0, c).start()
    first = Gather(peers, h1, (h1_send, h1_recv))
    third = Gather(peers, gm, (gm_send, gm_recv), lambda k: tok.at[k])

    def pass_h2(k):
        return remote(h2.at[k, 0], h2.at[k, 1], (h2_send, h2_recv), k, peers.beside)

    def pass_g(k):
        return remote(cotangent.at[k], g.at[k, 1], (g_send, g_recv), k, peers.beside)

    buffers = (lambda k: part.at[k, pl.ds(2, 2)], lambda k: part.at[k, 1], came, far)
    scatter_a = Scatter(peers, *buffers, (a_send, a_recv))
    scatter_c = Scatter(peers, *buffers, (c_send, c_recv))

    def pass_grad(k):
        return remote(part.at[k, 1], came.at[k, 0], (b_send, b_recv), 2 * k, peers.beside)

    def pass_result(k):
        return remote(part.at[k, 3], came.at[k, 1], (b_send, b_recv), 2 * k + 1, peers.beside)

    g1, g2, gh = gain_one[...], gain_two[...], gain_head[...]
    gains[...] = jnp.zeros_like(gains)
    head_part[...] = jnp.zeros_like(head_part)
    loads[0].wait()

    def norm_first(k):
        def some(r):
            _, _, hidden = normalize(tok[k, r].astype(F32), g1)
            h1[k, 0, r] = hidden

        by_rows(rows, some)
        first.start(k)

    loop(slots, norm_first)
    loop(slots, lambda k: pass_g(k).start())
    for t, c in ((1, 0), (1, 1), (1, 2), (2, 0), (2, 1), (3, 0)):
        weight_step(t, c)
    for one in loads[1:6]:
        one.wait()

    same = same_head(width)
    ones = same.astype(BF)

    def attend_all(qkvg, mixed_s, gated_s, state_s):
        def saves(k):
            return [
                pltpu.make_async_copy(qkvg, qkvg_hbm.at[k], save_sem.at[0]),
                pltpu.make_async_copy(mixed_s, mixed_hbm.at[k], save_sem.at[1]),
                pltpu.make_async_copy(gated_s, gated_hbm.at[k], save_sem.at[2]),
                pltpu.make_async_copy(state_s, state_hbm.at[k], save_sem.at[3]),
            ]

        def attend(k):
            first.forward(k)

            @pl.when(k > 0)
            def _():
                scatter_a.middle_step(k - 1)
                for one in saves(k - 1):
                    one.wait()

            @pl.when(k == 1)
            def _():
                weight_step(2, 2)
                weight_step(3, 1)

            @pl.when(k == 2)
            def _():
                weight_step(3, 2)

            first.arrived(k)
            state[...] = jnp.zeros_like(state)
            length = length_ref[k]

            def chunk(i):
                j = peers.relative(i)
                hidden = h1[k, j]
                position = lax.broadcasted_iota(jnp.int32, (rows, width), 0) + i * rows
                query = softplus(nn(hidden, w4[0])).astype(BF)
                keys = jnp.where(position < length, softplus(nn(hidden, w4[1])), 0.0).astype(BF)
                values = nn(hidden, w4[2]).astype(BF)
                gate = nn(hidden, w4[3])
                qkvg[j, 0] = query
                qkvg[j, 1] = keys
                qkvg[j, 2] = values
                qkvg[j, 3] = gate.astype(BF)
                before = state[...].astype(BF)
                state_s[i] = before
                scores = masked(nt(query, by_head(keys)), causal(rows, heads, False))
                mixed = nn(query, before) + nn(scores, by_head(values))
                state[...] += jnp.where(same, tn(keys, values), 0.0)
                mixed_s[j] = mixed.astype(BF)
                scale = lax.rsqrt(head_mean(mixed * mixed, ones) + EPS)
                gated_s[j] = (mixed * scale * gh * (gate * sigmoid(gate))).astype(BF)

            loop(BLOCKS, chunk)
            for one in saves(k):
                one.start()

            def project(p):
                j = (p % 2) * 2 + p // 2
                part[k, p] = nn(gated_s[j], wo_v[...]).astype(BF)

            project(2)
            project(3)
            scatter_a.start(k)
            project(1)
            project(0)

        loop(slots, attend)
        for one in saves(slots - 1):
            one.wait()

    pl.run_scoped(
        attend_all,
        v((BLOCKS, 4, rows, width), BF),
        v((BLOCKS, rows, width), BF),
        v((BLOCKS, rows, width), BF),
        v((BLOCKS, width, width), BF),
    )
    scatter_a.middle_step(slots - 1)

    def finish_attend(k):
        scatter_a.arrived(k)

        def some(r):
            value = (
                tok[k, r].astype(F32)
                + part[k, 0, r].astype(F32)
                + came[k, 0, r].astype(F32)
                + far[k, r].astype(F32)
            )
            middle[k, r] = value
            _, _, hidden = normalize(value, g2)
            h2[k, 0, r] = hidden

        by_rows(rows, some)
        pass_h2(k).start()
        scatter_a.sent(k)

    finish_attend(0)
    finish_attend(1)
    loads[6].wait()

    def result_save(k):
        return pltpu.make_async_copy(part.at[k, 2], result.at[k], save_sem.at[4 + k])

    def unit_all(mat, prod_s, gu_s, gp_s, staged):
        def mat_load(c, which):
            source = mats[c] if which == 0 else other.at[c]
            return pltpu.make_async_copy(
                source, mat.at[c, pl.ds(which * hid, hid)], mat_sem.at[2 * c + which]
            )

        for c in range(3):
            mat_load(c, 0).start()
        for c in range(3):
            weight_step(4, c)
            mat_load(c, 1).start()
        for c in range(3):
            mat_load(c, 0).wait()
            mat_load(c, 1).wait()

        def unit(k):
            pass_h2(k).wait_recv()
            pass_g(k).wait_recv()

            def one(t):
                j = 1 - t
                hidden, grad = h2[k, j], g[k, j]
                up_part = nt(hidden, mat[0])
                pair_part = nt(hidden, mat[1])
                product = (up_part * pair_part).astype(BF)
                prod_s[k, j] = product
                part[k, 2 + j] = nn(product, mat[2]).astype(BF)
                grad_product = nt(grad, mat[2]).astype(BF).astype(F32)
                grad_up = (grad_product * pair_part).astype(BF)
                grad_pair = (grad_product * up_part).astype(BF)
                gu_s[k, j] = grad_up
                gp_s[k, j] = grad_pair
                part[k, j] = (nn(grad_up, mat[0]) + nn(grad_pair, mat[1])).astype(BF)

                @pl.when(t == 0)
                def _():
                    pass_grad(k).start()
                    pass_result(k).start()

            loop(2, one)

            @pl.when(k == 0)
            def _():
                for m in range(2, slots):
                    finish_attend(m)

            pass_grad(k).wait_recv()
            pass_result(k).wait_recv()

            def some(r):
                value = middle[k, r]
                total = value + part[k, 2, r].astype(F32) + came[k, 1, r].astype(F32)
                part[k, 2, r] = total.astype(BF)
                grad = part[k, 0, r].astype(F32) + came[k, 0, r].astype(F32)
                normed, scale, _ = normalize(value, g2)
                gains[1:2] += jnp.sum(grad * normed, axis=0, keepdims=True)
                back = g[k, 0, r].astype(F32) + norm_back(grad, normed, scale, g2)
                middle[k, r] = back
                tok[k, r] = back.astype(BF)

            by_rows(rows, some)
            third.start(k)
            pltpu.make_async_copy(tok.at[k], gm.at[k, 0], save_sem.at[4 + slots + k]).start()
            result_save(k).start()

        loop(slots, unit)
        tile = 256
        everything = slots * 2 * rows

        def weigh(c, left, right):
            for start in range(0, both, tile):
                span = min(tile, both - start)
                term = tn(
                    left[:, :, :, start : start + span].reshape(everything, span),
                    right[...].reshape(everything, feat),
                ).astype(BF)
                for q in range(2):
                    for m in range(2):
                        base = q * hid + m * (hid // 2)
                        low, high = max(start, base), min(start + span, base + hid // 2)
                        if low >= high:
                            continue
                        for p in range(8):
                            index = q * 8 + p if KINDS["UPD"[c] if m == 0 else "upd"[c]][0] == "first" else p * 2 + q
                            staged[index, low - q * hid : high - q * hid] = term[
                                low - start : high - start, p * eighth : (p + 1) * eighth
                            ]
            save = pltpu.make_async_copy(staged, sums.at[c], save_sem.at[3])
            save.start()
            save.wait()
            for m in range(2):
                begin_unit(c, m)

        turn = iter(range(slots))
        for c in UNIT_ORDER:
            weigh(c, (gu_s, gp_s, prod_s)[c], (h2, h2, g)[c])
            third.forward(next(turn))
        for k in turn:
            third.forward(k)

    half = pl.ds(0, hid // 2), pl.ds(hid // 2, hid // 2)
    unit_sems = (
        ((u_send, u_recv), (p_send, p_recv), (d_send, d_recv)),
        ((u2_send, u2_recv), (p2_send, p2_recv), (d2_send, d2_recv)),
    )

    def unit_chain(c, m, work, room):
        across, bits = KINDS[("UPD", "upd")[m][c]]
        return Chain(
            peers, bits, work, unit_came.at[c, :, half[m]], room, unit_total.at[c, :, half[m]],
            unit_sems[m][c], chain_sem.at[0], sums.at[c, :, half[m]], unit_far.at[c, :, half[m]], across,
        )

    def begin_unit(c, m):
        unit_chain(c, m, h2.at[0], None).begin()

    pl.run_scoped(
        unit_all,
        v((3, both, feat), BF),
        v((slots, 2, rows, both), BF),
        v((slots, 2, rows, both), BF),
        v((slots, 2, rows, both), BF),
        v((16, hid, eighth), BF),
    )

    def rest(works, room, qk_work, vg_work, out_work, pair_room, small_room):
        chains = {}
        work_loads = []
        for m in range(2):
            for c in range(3):
                name = ("UPD", "upd")[m][c]
                work = works.at[c, :, half[m]]
                chains[name] = unit_chain(c, m, work, room)
                first_half = 0 if KINDS[name][0] == "first" else peers.bit(KINDS[name][1][0]) * 8
                work_loads.append(
                    pltpu.make_async_copy(
                        sums.at[c, pl.ds(first_half, 8), half[m]], work, mat_sem.at[3 * m + c]
                    )
                )
        for name, work, come, space, total, pair_sems in (
            ("Q", qk_work, qk_came, pair_room, qk_total, (q_send, q_recv)),
            ("V", vg_work, vg_came, pair_room, vg_total, (v_send, v_recv)),
            ("O", out_work, out_came, small_room, out_total, (o_send, o_recv)),
        ):
            chains[name] = Chain(
                peers, KINDS[name][1], work, come, space, total, pair_sems, chain_sem.at[0]
            )
        for one in work_loads:
            one.start()
        for one in work_loads:
            one.wait()
        done = {name: 0 for name in chains}
        plan, tail, where = {}, [], (0, -1)
        for name, at in SCHEDULE:
            if name == "c":
                where = (at // 10, at % 10 + 1)
            elif name == "g":
                where = (at, 0)
            elif name == "T":
                where = None
            elif name in chains and where is None or name in ("F", "B", "A"):
                tail.append((name, at))
            elif name in chains:
                slot, point = where
                if point == 8 and slot + 1 < slots:
                    slot, point = slot + 1, -1
                plan.setdefault((slot, point), []).append((name, at))

        def play(actions):
            for name, stage in actions:
                chains[name].step(stage)
                done[name] = max(done[name], stage + 1)

        def attend_all_back(qkvg, mixed_v, state_v, gated, gm_v, pre, acc, out_acc):
            def slot_loads(k):
                b = k % 2
                pairs = (
                    (qkvg_hbm, qkvg), (mixed_hbm, mixed_v), (state_hbm, state_v), (gated_hbm, gated)
                )
                return [
                    pltpu.make_async_copy(source.at[k], target.at[b], slot_sem.at[4 * b + m])
                    for m, (source, target) in enumerate(pairs)
                ]

            for one in slot_loads(0):
                one.start()

            def hooks(k, point, low, high):
                for (slot, at), actions in plan.items():
                    if not low <= at < high:
                        continue

                    @pl.when((k == slot) & (point == at))
                    def _():
                        play(actions)

            def attend_back(k):
                b = k % 2
                hooks(k, -1, -1, 0)
                hooks(k, 0, 0, 1)
                third.arrived(k)
                pltpu.make_async_copy(tok.at[k], gm.at[k, 0], save_sem.at[4 + slots + k]).wait()
                fetch = pltpu.make_async_copy(gm.at[k], gm_v, slot_sem.at[8])
                fetch.start()

                @pl.when(k > 0)
                def _():
                    scatter_c.middle_step(k - 1)

                @pl.when(k + 1 < slots)
                def _():
                    for one in slot_loads(k + 1):
                        one.start()

                for one in slot_loads(k):
                    one.wait()
                result_save(k).wait()
                pass_grad(k).wait_send()
                pass_result(k).wait_send()
                state[...] = jnp.zeros_like(state)
                fetch.wait()

                def chunk(step):
                    hooks(k, step, 1, BLOCKS)
                    i = BLOCKS - 1 - step
                    j = peers.relative(i)
                    grad_gated = nt(gm_v[j], wo_v[...]).astype(BF).astype(F32)
                    query, keys, values = qkvg[b, j, 0], qkvg[b, j, 1], qkvg[b, j, 2]
                    gate = qkvg[b, j, 3].astype(F32)
                    mixed = mixed_v[b, j].astype(F32)
                    scale = lax.rsqrt(head_mean(mixed * mixed, ones) + EPS)
                    normed = mixed * scale
                    opened = sigmoid(gate)
                    grad_gate = grad_gated * (normed * gh) * opened * (1.0 + gate * (1.0 - opened))
                    grad_head = grad_gated * (gate * opened)
                    head_part[...] += jnp.sum(grad_head * normed, axis=0, keepdims=True)
                    scaled = grad_head * gh
                    inner = head_mean(scaled * normed, ones)
                    grad_mixed = (scale * (scaled - normed * inner)).astype(BF)
                    after = state[...].astype(BF)
                    before = state_v[b, i]
                    lower = causal(rows, heads, False)
                    upper = causal(rows, heads, True)
                    query_heads = by_head(query)
                    mixed_heads = by_head(grad_mixed)
                    grad_scores = masked(nt(grad_mixed, by_head(values)), lower)
                    grad_query = nt(grad_mixed, before) + nn(grad_scores, by_head(keys))
                    grad_scores_t = masked(nt(values, mixed_heads), upper)
                    grad_keys = nt(values, after) + nn(grad_scores_t, query_heads)
                    scores_t = masked(nt(keys, query_heads), upper)
                    grad_values = nn(keys, after) + nn(scores_t, mixed_heads)
                    state[...] += jnp.where(same, tn(query, grad_mixed), 0.0)

                    rounded = lambda x: x.astype(BF).astype(F32)
                    pre_q = (rounded(grad_query) * sigmoid_of_softplus(query.astype(F32))).astype(BF)
                    pre_k = (rounded(grad_keys) * sigmoid_of_softplus(keys.astype(F32))).astype(BF)
                    pre_v = grad_values.astype(BF)
                    pre_g = grad_gate.astype(BF)
                    for m, one in enumerate((pre_q, pre_k, pre_v, pre_g)):
                        pre[j, :, m * width : (m + 1) * width] = one
                    grad_h = (
                        nt(pre_q, w4[0]) + nt(pre_k, w4[1]) + nt(pre_v, w4[2]) + nt(pre_g, w4[3])
                    )
                    part[k, spot(j)] = grad_h.astype(BF)

                loop(BLOCKS, chunk)
                scatter_c.start(k)
                pre_all = pre[...].reshape(BLOCKS * rows, 4 * width)

                def weigh(m):
                    hooks(k, BLOCKS + m, BLOCKS, 8)
                    cols = pl.ds(pl.multiple_of(m * 256, 256), 256)
                    term = tn(h1[k, :, :, cols].reshape(BLOCKS * rows, 256), pre_all)
                    acc[cols] = jnp.where(k > 0, acc[cols], 0.0) + term

                loop(feat // 256, weigh)
                term = tn(gated[b].reshape(BLOCKS * rows, width), gm_v[...].reshape(BLOCKS * rows, feat))
                out_acc[...] = jnp.where(k > 0, out_acc[...], 0.0) + term

            loop(slots, attend_back)
            play(plan.get((slots - 1, 8), ()))
            scatter_c.middle_step(slots - 1)
            part_rows = width // 8

            def fill(p):
                at = pl.ds(pl.multiple_of(p * eighth, eighth), eighth)
                small = pl.ds(pl.multiple_of(p * part_rows, part_rows), part_rows)
                qk_work[p] = acc[at, : 2 * width].astype(BF)
                vg_work[p] = acc[at, 2 * width :].astype(BF)
                out_work[p] = out_acc[small].astype(BF)

            loop(8, fill)
            for name in ATTENTION_ORDER:
                chains[name].begin()

        pl.run_scoped(
            attend_all_back,
            v((2, BLOCKS, 4, rows, width), BF),
            v((2, BLOCKS, rows, width), BF),
            v((2, BLOCKS, width, width), BF),
            v((2, BLOCKS, rows, width), BF),
            v((BLOCKS, rows, feat), BF),
            v((BLOCKS, rows, 4 * width), BF),
            v((feat, 4 * width), F32),
            v((width, feat), F32),
        )
        loop(slots, lambda k: third.sent(k))
        again = load(tokens, tok, 0)
        again.start()

        def grad_save(k):
            return pltpu.make_async_copy(middle.at[k], grad_tokens.at[k], save_sem.at[4 + k])

        def finish(k):
            scatter_c.arrived(k)

            def some(r):
                grad = (
                    part[k, 0, r].astype(F32) + came[k, 0, r].astype(F32) + far[k, r].astype(F32)
                )
                normed, scale, _ = normalize(tok[k, r].astype(F32), g1)
                gains[0:1] += jnp.sum(grad * normed, axis=0, keepdims=True)
                middle[k, r] = middle[k, r] + norm_back(grad, normed, scale, g1)

            by_rows(rows, some)
            grad_save(k).start()

        others = [peers.beside, peers.across] + [peers.partner(h) for h in range(peers.hops)]

        def gain_hop(t):
            return remote(gains, gain_came.at[t], (gain_send, gain_recv), t, others[t])

        def gain_begin():
            lane = lax.broadcasted_iota(jnp.int32, (1, BLOCKS * width), 1) // width
            spread = jnp.concatenate([head_part[...]] * BLOCKS, axis=1)
            gains[2:3] = jnp.where(lane == peers.place, spread, 0.0)
            gain_hop(0).start()

        hop = iter(range(len(others)))

        def gain_step():
            t = next(hop, None)
            if t is None:
                return
            gain_hop(t).wait_recv()
            gain_hop(t).wait_send()
            gains[...] += gain_came[t]
            if t + 1 < len(others):
                gain_hop(t + 1).start()

        again.wait()
        turn = iter(range(slots))
        for name, stage in tail:
            if name == "F":
                finish(next(turn))
            elif name == "B":
                for k in turn:
                    finish(k)
                gain_begin()
            elif name == "A":
                gain_step()
            else:
                play([(name, stage)])
        for _ in others:
            gain_step()
        most = max(one.count for one in chains.values())
        for t in range(most):
            for name in chains:
                if done[name] <= t < chains[name].count:
                    play([(name, t)])
        for one in chains.values():
            one.sent()

        def settle(k):
            grad_save(k).wait()
            first.sent(k)
            scatter_c.sent(k)
            pass_h2(k).wait_send()
            pass_g(k).wait_send()

        loop(slots, settle)

        def settle_weights(c):
            for t in range(4):
                weight_hop(t, c).wait_send()

        for c in range(3):
            settle_weights(c)

    pl.run_scoped(
        rest,
        v((3, 8, hid, eighth), BF),
        v((8, hid // 2, eighth), BF),
        v((8, eighth, 2 * width), BF),
        v((8, eighth, 2 * width), BF),
        v((8, width // 8, feat), BF),
        v((4, eighth, 2 * width), BF),
        v((4, width // 8, feat), BF),
    )


def dma(n):
    return pltpu.SemaphoreType.DMA((n,))


def anywhere(n):
    return [pl.BlockSpec(memory_space=pl.ANY)] * n


def in_vmem(n):
    return [pl.BlockSpec(memory_space=pltpu.VMEM)] * n


KINDS = {
    "U": ("first", (0, 1, 2)),
    "P": ("last", (0, 1, 2)),
    "D": ("first", (0, 1, 2)),
    "u": ("last", (1, 0, 2)),
    "p": ("last", (0, 1, 2)),
    "d": ("first", (0, 1, 2)),
    "Q": (None, (0, 1, 2)),
    "V": (None, (1, 0, 2)),
    "O": (None, (0, 1, 2)),
}
UNIT_ORDER = (1, 0, 2)
ATTENTION_ORDER = ('O', 'V', 'Q')
SCHEDULE = (
    ("P", 0), ("g", 0), ("c", 0), ("U", 0), ("u", 0), ("c", 1), ("p", 0), ("P", 1), ("c", 2), ("c", 3),
    ("c", 4), ("U", 1), ("D", 0), ("p", 1), ("c", 5), ("c", 6), ("P", 2), ("c", 7), ("u", 1), ("g", 1),
    ("U", 2), ("c", 10), ("p", 2), ("D", 1), ("c", 11), ("d", 0), ("P", 3), ("u", 2), ("c", 12), ("U", 3),
    ("D", 2), ("c", 13), ("P", 4), ("c", 14), ("d", 1), ("c", 15), ("p", 3), ("U", 4), ("c", 16), ("P", 5),
    ("u", 3), ("c", 17), ("D", 3), ("g", 2), ("p", 4), ("d", 2), ("c", 20), ("c", 21), ("U", 5), ("c", 22),
    ("D", 4), ("c", 23), ("c", 24), ("p", 5), ("c", 25), ("d", 3), ("c", 26), ("c", 27), ("T", 0), ("F", 0),
    ("F", 1), ("O", 0), ("d", 4), ("F", 2), ("B", 0), ("V", 0), ("u", 4), ("D", 5), ("A", 0), ("O", 1),
    ("A", 0), ("A", 0), ("Q", 0), ("A", 0), ("O", 2), ("A", 0), ("V", 1), ("Q", 1), ("d", 5), ("O", 3),
    ("V", 2), ("O", 4), ("Q", 2), ("u", 5), ("V", 3), ("Q", 3), ("V", 4), ("Q", 4),
)


def block(batch, lengths, tokens, cotangent, q4, wo, up, pair, down, gain_one, gain_two, gain_head):
    slots, rows, feat = tokens.shape
    width, hid = wo.shape[0], down.shape[0]
    eighth = feat // 8
    n = BLOCKS
    hops = batch.bit_length() - 1
    extra = hops - 3
    shape = jax.ShapeDtypeStruct
    blocks = lambda *dims: shape((slots, n) + dims, BF)
    outs = [
        shape((slots, rows, feat), BF),
        shape((slots, rows, feat), F32),
        shape((3, 8, hid, eighth), BF),
        shape((8, eighth, 2 * width), BF),
        shape((8, eighth, 2 * width), BF),
        shape((8, width // 8, feat), BF),
        shape((3, feat), F32),
        blocks(4, rows, width),
        blocks(rows, width),
        blocks(rows, width),
        blocks(width, width),
        blocks(rows, feat),
        shape((3, hid, feat), BF),
        shape((3, 16, hid, eighth), BF),
        shape((3, 14 + 2 * extra, hid, eighth), BF),
        shape((3, 8, hid, eighth), BF),
        shape((7 + extra, eighth, 2 * width), BF),
        shape((7 + extra, eighth, 2 * width), BF),
        shape((7 + extra, width // 8, feat), BF),
    ]
    v = pltpu.VMEM
    scratch = [
        v((slots, rows, feat), BF),
        v((4, feat, width), BF),
        v((width, feat), BF),
        v((slots, n, rows, feat), BF),
        v((slots, 2, rows, feat), BF),
        v((slots, 2, rows, feat), BF),
        v((slots, n, rows, feat), BF),
        v((slots, 2, rows, feat), BF),
        v((slots, rows, feat), BF),
        v((slots, rows, feat), F32),
        v((width, width), F32),
        v((hops + 2, 3, feat), F32),
        v((1, width), F32),
        dma(7),
        dma(4 + 2 * slots),
        dma(9),
        dma(6),
        dma(1),
        *[dma(3 * slots)] * 4,
        *[dma(slots)] * 4,
        *[dma(12)] * 2,
        *[dma(2 * slots)] * 6,
        *[dma(hops + 2)] * 2,
        *[dma(7 + extra)] * 18,
    ]
    total = slots * n * rows
    return pl.pallas_call(
        functools.partial(block_kernel, batch),
        in_specs=[pl.BlockSpec(memory_space=pltpu.SMEM)] + anywhere(10) + in_vmem(3),
        out_specs=anywhere(6) + in_vmem(1) + anywhere(12),
        out_shape=outs,
        scratch_shapes=scratch,
        compiler_params=pltpu.CompilerParams(
            collective_id=1, has_side_effects=True, vmem_limit_bytes=VMEM_LIMIT
        ),
        cost_estimate=pl.CostEstimate(
            flops=total * (30 * feat * width + 56 * width * width + 18 * feat * hid),
            transcendentals=total * 12 * width,
            bytes_accessed=2 * total * (12 * feat + 3 * hid),
        ),
        name="block",
    )(lengths, tokens, cotangent, *q4, wo, up, pair, down, gain_one, gain_two, gain_head)


def widen_kernel(unit, qk, vg, out, *targets):
    width = qk.shape[2] // 2
    for c in range(3):
        targets[5 + c][...] = unit[c, 0].astype(F32)
    targets[0][...] = qk[0, :, :width].astype(F32)
    targets[1][...] = qk[0, :, width:].astype(F32)
    targets[2][...] = vg[0, :, :width].astype(F32)
    targets[3][...] = vg[0, :, width:].astype(F32)
    targets[4][...] = out[0].astype(F32)


def widen(unit, qk, vg, out):
    hid, eighth = unit.shape[2:]
    width, feat = qk.shape[2] // 2, 8 * eighth
    piece = lambda dims: pl.BlockSpec((1,) + dims, lambda i: (i, 0, 0))
    flat = lambda dims: pl.BlockSpec(dims, lambda i: (i, 0))
    whole = lambda rows, cols: jax.ShapeDtypeStruct((rows, cols), F32)
    return pl.pallas_call(
        widen_kernel,
        grid=(8,),
        in_specs=[
            pl.BlockSpec((3, 1, hid, eighth), lambda i: (0, i, 0, 0)),
            piece(qk.shape[1:]),
            piece(vg.shape[1:]),
            piece(out.shape[1:]),
        ],
        out_specs=[flat((eighth, width))] * 4
        + [flat((width // 8, feat))]
        + [pl.BlockSpec((hid, eighth), lambda i: (0, i))] * 3,
        out_shape=[whole(feat, width)] * 4 + [whole(width, feat)] + [whole(hid, feat)] * 3,
        compiler_params=pltpu.CompilerParams(vmem_limit_bytes=VMEM_LIMIT),
        name="widen",
    )(unit, qk, vg, out)


def on_device(
    batch,
    tokens,
    lengths,
    assignment,
    query_weight,
    key_weight,
    value_weight,
    gate_weight,
    out_weight,
    up_weight,
    pair_weight,
    down_weight,
    attention_norm_gain,
    mlp_gain,
    head_gain,
    cotangent,
):
    slots = tokens.shape[0]
    width = query_weight.shape[1]
    place = lax.axis_index("seq").astype(jnp.int32)
    seq_ids = lax.broadcasted_iota(jnp.int32, (slots, lengths.shape[0]), 1)
    slot_length = jnp.sum(jnp.where(assignment[:, None] == seq_ids, lengths[None, :], 0), axis=1)
    q4 = (query_weight, key_weight, value_weight, gate_weight)
    gain_one, gain_two, gain_head = attention_norm_gain[None], mlp_gain[None], head_gain[None]
    result, grad_inputs, unit_total, qk_total, vg_total, out_total, gains = block(
        batch, slot_length, tokens, cotangent, q4, out_weight, up_weight.T, pair_weight.T, down_weight,
        gain_one, gain_two, gain_head,
    )[:7]
    grad_qw, grad_kw, grad_vw, grad_gw, grad_outw, grad_upw, grad_pairw, grad_down = widen(
        unit_total, qk_total, vg_total, out_total
    )
    head_total = lax.dynamic_slice(gains[2], (place * width,), (width,))
    return (
        result,
        grad_inputs,
        grad_qw,
        grad_kw,
        grad_vw,
        grad_gw,
        grad_outw,
        grad_upw.T,
        grad_pairw.T,
        grad_down,
        gains[0],
        gains[1],
        head_total,
    )


def solution(mesh):
    return jax.shard_map(
        functools.partial(on_device, mesh.shape["batch"]),
        mesh=mesh,
        in_specs=(
            P("batch", "seq", None),
            P(),
            P("batch"),
            P(None, "seq"),
            P(None, "seq"),
            P(None, "seq"),
            P(None, "seq"),
            P("seq", None),
            P(None, "seq"),
            P(None, "seq"),
            P("seq", None),
            P(),
            P(),
            P("seq"),
            P("batch", "seq", None),
        ),
        out_specs=(
            P("batch", "seq", None),
            P("batch", "seq", None),
            P(None, "seq"),
            P(None, "seq"),
            P(None, "seq"),
            P(None, "seq"),
            P("seq", None),
            P(None, "seq"),
            P(None, "seq"),
            P("seq", None),
            P(),
            P(),
            P("seq"),
        ),
        check_vma=False,
    )
```

time: 1110 us -> 345 us (0.31)
  waiting for transfers between devices: 729 us -> 0 us
  Pallas kernels: 0 us -> 335 us
  matrix products: 209 us -> 0 us
  blocking collectives: 59.7 us -> 0 us
  other arithmetic: 48.2 us -> 1.36 us
  local copies, waits for them, and re-layouts: 42.2 us -> 5.51 us
  between operations: 14.6 us -> 0.69 us
    psum x1 -> x0, waiting for transfers between devices: 437 us -> none  [on_device(): lax.psum((grad_qw, grad_kw, grad_vw, grad_gw, grad_outw, grad_upw, grad_p...]
    pallas_call x0 -> x2, Pallas kernels: none -> 335 us  [the longest x1 326 us: block(): pl.pallas_call(functools.partial(block_kernel, batch), in_specs=[pl.Block...]
    dot_general x30 -> x0, matrix products: 209 us -> none  [the longest x5 48.4 us: weight_grad(): lax.dot_general(inputs, grads, (((0, 1), (0, 1)), ((), ())), preferred_el...]
    all_gather x4 -> x0, waiting for transfers between devices: 175 us -> none  [the longest x1 46.5 us: on_device(): lax.all_gather(grad_middle.astype(jnp.bfloat16), 'seq', axis=0, tiled=True)]
    reduce_scatter x4 -> x0, waiting for transfers between devices: 116 us -> none  [the longest x1 58.3 us: on_device(): lax.psum_scatter((matmul_back(grad_up, up_weight) + matmul_back(grad_pair...]
    psum x2 -> x0, blocking collectives: 59.7 us -> none  [the longest x1 37.4 us: on_device(): lax.psum((gain_one_part, gain_two_part), ('batch', 'seq'))]
    unnamed x134 -> x6, local copies, waits for them, and re-layouts: 26 us -> 4.34 us
    convert_element_type x6 -> x0, other arithmetic: 17.4 us -> none  [the longest x1 5.11 us: on_device(): keys = (jax.nn.softplus(pre_key) * valid[..., None]).astype(jnp.bfloat16)]
  transfers between devices with their start and end apart: 9 -> 0, of which waited for: 7 -> 0; matrix products, arithmetic and copies ran while one was open for 8% -> 0% of each run, Pallas kernels for 0% -> 0%
where the time goes in v3:
time: 345 us; the launch traced here: 343 us
  Pallas kernels  335 us (97%)
  local copies, waits for them, and re-layouts  5.51 us (2%)
    pallas_call x1, Pallas kernels, block(): pl.pallas_call(functools.partial(block_kernel, batch), in_specs=[pl.Block...  326 us
    pallas_call x1, Pallas kernels, widen(): pl.pallas_call(widen_kernel, grid=(8,), in_specs=[pl.BlockSpec((3, 1, hid...  8.89 us

profile of v3, /device:TPU:0, one launch (start us, length us, event | category | flops | bytes accessed | tf_op | source)
XLA Modules:
  0.0 342.9 jit_solution(12947696606353921099)
XLA Ops:
  0.6 1.4 select_reduce_fusion.length_ref
  2.0 326.4 %block.1 = (bf16[3,256,1024]{2,1,0:T(8,128)(2,1)}, f32[3,256,1024]{2,1,0:T(8,128)}, bf16[3,8,704,128]{3,2,1,0:T(8,128)(2,1)}, bf16[8,128,512]{2,1,0:T(8,128)(2,1...) custom-call(s32[3]{0:T(128)} %select_reduce_fusion.length_ref, ...), custom_call_target="tpu_custom_call" | custom-call | flops 75296145408 | bytes 88473600 | tf_op jit(solution)/shard_map/block/pallas_call | solution.py:1007
  328.4 0.0 copy-start.1
  328.4 8.9 %widen.1 = (f32[1024,256]{1,0:T(8,128)}, f32[1024,256]{1,0:T(8,128)}, f32[1024,256]{1,0:T(8,128)}, f32[1024,256]{1,0:T(8,128)}, f32[256,1024]{1,0:T(8,128)}, /*i...) custom-call(bf16[3,8,704,128]{3,2,1,0:T(8,128)(2,1)} %get-tuple-element.30.unit, ...), custom_call_target="tpu_custom_call" | custom-call | tf_op jit(solution)/shard_map/widen/pallas_call | solution.py:1042
  337.3 0.0 copy-start
  337.3 0.0 copy-done.1
  337.3 0.6 fusion
  338.0 0.6 constant_dynamic-slice_fusion
  338.5 2.7 copy.30
  341.2 0.0 copy-done
  341.2 1.7 copy.31
Async XLA Ops:
  328.4 8.9 %copy-start.1 = (f32[3,1024]{1,0:T(4,128)S(1)}, f32[3,1024]{1,0:T(4,128)}, u32[]{:S(2)}) copy-start(f32[3,1024]{1,0:T(4,128)} %get-tuple-element.42) | copy-start | bytes 36868
  337.3 3.9 %copy-start = (f32[3,256,1024]{2,1,0:T(8,128)S(1)}, f32[3,256,1024]{2,1,0:T(8,128)}, u32[]{:S(2)}) copy-start(f32[3,256,1024]{2,1,0:T(8,128)} %get-tuple-element.60) | copy-start | bytes 9437188

commit v4 on v3

--- a/solution.py
+++ b/solution.py
@@ -921,28 +921,28 @@
 
 
 KINDS = {
-    "U": ("first", (0, 1, 2)),
-    "P": ("last", (0, 1, 2)),
+    "U": ("last", (0, 1, 2)),
+    "P": ("first", (0, 1, 2)),
     "D": ("first", (0, 1, 2)),
     "u": ("last", (1, 0, 2)),
-    "p": ("last", (0, 1, 2)),
-    "d": ("first", (0, 1, 2)),
-    "Q": (None, (0, 1, 2)),
-    "V": (None, (1, 0, 2)),
+    "p": ("first", (0, 1, 2)),
+    "d": ("last", (1, 0, 2)),
+    "Q": (None, (1, 0, 2)),
+    "V": (None, (0, 1, 2)),
     "O": (None, (0, 1, 2)),
 }
-UNIT_ORDER = (1, 0, 2)
-ATTENTION_ORDER = ('O', 'V', 'Q')
+UNIT_ORDER = (0, 1, 2)
+ATTENTION_ORDER = ('O', 'Q', 'V')
 SCHEDULE = (
-    ("P", 0), ("g", 0), ("c", 0), ("U", 0), ("u", 0), ("c", 1), ("p", 0), ("P", 1), ("c", 2), ("c", 3),
-    ("c", 4), ("U", 1), ("D", 0), ("p", 1), ("c", 5), ("c", 6), ("P", 2), ("c", 7), ("u", 1), ("g", 1),
-    ("U", 2), ("c", 10), ("p", 2), ("D", 1), ("c", 11), ("d", 0), ("P", 3), ("u", 2), ("c", 12), ("U", 3),
-    ("D", 2), ("c", 13), ("P", 4), ("c", 14), ("d", 1), ("c", 15), ("p", 3), ("U", 4), ("c", 16), ("P", 5),
-    ("u", 3), ("c", 17), ("D", 3), ("g", 2), ("p", 4), ("d", 2), ("c", 20), ("c", 21), ("U", 5), ("c", 22),
-    ("D", 4), ("c", 23), ("c", 24), ("p", 5), ("c", 25), ("d", 3), ("c", 26), ("c", 27), ("T", 0), ("F", 0),
-    ("F", 1), ("O", 0), ("d", 4), ("F", 2), ("B", 0), ("V", 0), ("u", 4), ("D", 5), ("A", 0), ("O", 1),
-    ("A", 0), ("A", 0), ("Q", 0), ("A", 0), ("O", 2), ("A", 0), ("V", 1), ("Q", 1), ("d", 5), ("O", 3),
-    ("V", 2), ("O", 4), ("Q", 2), ("u", 5), ("V", 3), ("Q", 3), ("V", 4), ("Q", 4),
+    ("u", 0), ("U", 0), ("g", 0), ("P", 0), ("c", 0), ("c", 1), ("u", 1), ("c", 2), ("c", 3), ("P", 1),
+    ("p", 0), ("U", 1), ("c", 4), ("u", 2), ("c", 5), ("c", 6), ("P", 2), ("c", 7), ("p", 1), ("g", 1),
+    ("D", 0), ("u", 3), ("p", 2), ("c", 10), ("c", 11), ("u", 4), ("c", 12), ("D", 1), ("p", 3), ("c", 13),
+    ("c", 14), ("D", 2), ("c", 15), ("p", 4), ("c", 16), ("c", 17), ("g", 2), ("P", 3), ("u", 5), ("p", 5),
+    ("d", 0), ("D", 3), ("c", 20), ("P", 4), ("c", 21), ("c", 22), ("c", 23), ("D", 4), ("c", 24), ("c", 25),
+    ("P", 5), ("d", 1), ("c", 26), ("c", 27), ("T", 0), ("U", 2), ("F", 0), ("d", 2), ("F", 1), ("O", 0),
+    ("F", 2), ("B", 0), ("U", 3), ("Q", 0), ("O", 1), ("d", 3), ("V", 0), ("U", 4), ("D", 5), ("A", 0),
+    ("O", 2), ("A", 0), ("Q", 1), ("A", 0), ("V", 1), ("A", 0), ("A", 0), ("U", 5), ("O", 3), ("Q", 2),
+    ("d", 4), ("V", 2), ("O", 4), ("d", 5), ("Q", 3), ("V", 3), ("Q", 4), ("V", 4),
 )
 
 
@@ -1022,10 +1022,14 @@
     )(lengths, tokens, cotangent, *q4, wo, up, pair, down, gain_one, gain_two, gain_head)
 
 
-def widen_kernel(unit, qk, vg, out, *targets):
+def widen_kernel(unit, qk, vg, out, first_in, second_in, *targets):
+    targets[8][...] = first_in[...]
+    targets[9][...] = second_in[...]
     width = qk.shape[2] // 2
+    eighth = unit.shape[3]
     for c in range(3):
-        targets[5 + c][...] = unit[c, 0].astype(F32)
+        for p in range(8):
+            targets[5 + c][:, p * eighth : (p + 1) * eighth] = unit[c, p].astype(F32)
     targets[0][...] = qk[0, :, :width].astype(F32)
     targets[1][...] = qk[0, :, width:].astype(F32)
     targets[2][...] = vg[0, :, :width].astype(F32)
@@ -1033,28 +1037,36 @@
     targets[4][...] = out[0].astype(F32)
 
 
-def widen(unit, qk, vg, out):
+def widen(unit, qk, vg, out, first, second):
     hid, eighth = unit.shape[2:]
     width, feat = qk.shape[2] // 2, 8 * eighth
     piece = lambda dims: pl.BlockSpec((1,) + dims, lambda i: (i, 0, 0))
     flat = lambda dims: pl.BlockSpec(dims, lambda i: (i, 0))
     whole = lambda rows, cols: jax.ShapeDtypeStruct((rows, cols), F32)
+    slots, rows, _ = first.shape
+    through = [pl.BlockSpec((slots, rows // 8, feat), lambda i: (0, i, 0))] * 2
+    like = lambda x: jax.ShapeDtypeStruct(x.shape, x.dtype)
     return pl.pallas_call(
         widen_kernel,
         grid=(8,),
         in_specs=[
-            pl.BlockSpec((3, 1, hid, eighth), lambda i: (0, i, 0, 0)),
+            pl.BlockSpec((3, 8, hid // 8, eighth), lambda i: (0, 0, i, 0)),
             piece(qk.shape[1:]),
             piece(vg.shape[1:]),
             piece(out.shape[1:]),
-        ],
+        ]
+        + through,
         out_specs=[flat((eighth, width))] * 4
         + [flat((width // 8, feat))]
-        + [pl.BlockSpec((hid, eighth), lambda i: (0, i))] * 3,
-        out_shape=[whole(feat, width)] * 4 + [whole(width, feat)] + [whole(hid, feat)] * 3,
+        + [flat((hid // 8, feat))] * 3
+        + through,
+        out_shape=[whole(feat, width)] * 4
+        + [whole(width, feat)]
+        + [whole(hid, feat)] * 3
+        + [like(first), like(second)],
         compiler_params=pltpu.CompilerParams(vmem_limit_bytes=VMEM_LIMIT),
         name="widen",
-    )(unit, qk, vg, out)
+    )(unit, qk, vg, out, first, second)
 
 
 def on_device(
@@ -1086,9 +1098,9 @@
         batch, slot_length, tokens, cotangent, q4, out_weight, up_weight.T, pair_weight.T, down_weight,
         gain_one, gain_two, gain_head,
     )[:7]
-    grad_qw, grad_kw, grad_vw, grad_gw, grad_outw, grad_upw, grad_pairw, grad_down = widen(
-        unit_total, qk_total, vg_total, out_total
-    )
+    (
+        grad_qw, grad_kw, grad_vw, grad_gw, grad_outw, grad_upw, grad_pairw, grad_down, result, grad_inputs,
+    ) = widen(unit_total, qk_total, vg_total, out_total, result, grad_inputs)
     head_total = lax.dynamic_slice(gains[2], (place * width,), (width,))
     return (
         result,

time: 345 us -> 337 us (0.977)
  local copies, waits for them, and re-layouts: 5.51 us -> 1.17 us
    pallas_call x1, Pallas kernels: 326 us -> 320 us  [block(): pl.pallas_call(functools.partial(block_kernel, batch), in_specs=[pl.Block...]
    unnamed x6 -> x2, local copies, waits for them, and re-layouts: 4.34 us -> 0.01 us
where the time goes in v4:
time: 337 us; the launch traced here: 335 us
  Pallas kernels  332 us (99%)
    pallas_call x1, Pallas kernels, block(): pl.pallas_call(functools.partial(block_kernel, batch), in_specs=[pl.Block...  320 us
    pallas_call x1, Pallas kernels, widen(): pl.pallas_call(widen_kernel, grid=(8,), in_specs=[pl.BlockSpec((3, 8, hid...  11.9 us

profile of v4, /device:TPU:0, one launch (start us, length us, event | category | flops | bytes accessed | tf_op | source)
XLA Modules:
  0.0 335.0 jit_solution(5389045515767271073)
XLA Ops:
  0.6 1.4 select_reduce_fusion.length_ref
  2.0 319.9 %block.1 = (bf16[3,256,1024]{2,1,0:T(8,128)(2,1)}, f32[3,256,1024]{2,1,0:T(8,128)}, bf16[3,8,704,128]{3,2,1,0:T(8,128)(2,1)}, bf16[8,128,512]{2,1,0:T(8,128)(2,1...) custom-call(s32[3]{0:T(128)} %select_reduce_fusion.length_ref, ...), custom_call_target="tpu_custom_call" | custom-call | flops 75296145408 | bytes 88473600 | tf_op jit(solution)/shard_map/block/pallas_call | solution.py:1007
  321.9 0.0 copy-start
  321.9 11.9 %widen.1 = (f32[1024,256]{1,0:T(8,128)}, f32[1024,256]{1,0:T(8,128)}, f32[1024,256]{1,0:T(8,128)}, f32[1024,256]{1,0:T(8,128)}, f32[256,1024]{1,0:T(8,128)}, /*i...) custom-call(bf16[3,8,704,128]{3,2,1,0:T(8,128)(2,1)} %get-tuple-elem, ...), custom_call_target="tpu_custom_call" | custom-call | tf_op jit(solution)/shard_map/widen/pallas_call | solution.py:1049
  333.8 0.0 copy-done
  333.8 0.6 fusion
  334.4 0.6 constant_dynamic-slice_fusion
Async XLA Ops:
  321.9 11.9 %copy-start = (f32[3,1024]{1,0:T(4,128)S(1)}, f32[3,1024]{1,0:T(4,128)}, u32[]{:S(2)}) copy-start(f32[3,1024]{1,0:T(4,128)} %get-tuple-element.46) | copy-start | bytes 36868

commit v5 on v4

--- a/solution.py
+++ b/solution.py
@@ -178,7 +178,7 @@
 
 
 class Chain:
-    def __init__(self, peers, bits, work, came, room, total, sems, load, source=None, far=None, across=None):
+    def __init__(self, peers, bits, work, came, room, total, sems, load, keep, source=None, far=None, across=None):
         self.peers, self.sems, self.stages, self.waited = peers, sems, [], set()
         b0, b1, b2 = (peers.bit(h) for h in bits)
         pair = 2 if across == "last" else 1
@@ -240,7 +240,7 @@
         if across == "last":
             self.stages.append((work.at[pl.ds(kept + 1, 1)], far.at[pl.ds(0, 1)], peers.across, meet))
         self.local = lambda: pltpu.make_async_copy(
-            work.at[pl.ds(kept, 1)], total.at[pl.ds(piece, 1)], load
+            work.at[pl.ds(kept, 1)], total.at[pl.ds(piece, 1)], keep
         )
         for where, h in (
             (pl.ds(piece, 1), bits[2]),
@@ -264,9 +264,9 @@
             self.hop(t).wait_send()
         self.stages[t][3]()
         if t == self.count - 4:
-            own = self.local()
-            own.start()
-            own.wait()
+            self.local().start()
+        if t == self.count - 3:
+            self.local().wait()
         if t + 1 < self.count:
             self.hop(t + 1).start()
 
@@ -617,7 +617,8 @@
         across, bits = KINDS[("UPD", "upd")[m][c]]
         return Chain(
             peers, bits, work, unit_came.at[c, :, half[m]], room, unit_total.at[c, :, half[m]],
-            unit_sems[m][c], chain_sem.at[0], sums.at[c, :, half[m]], unit_far.at[c, :, half[m]], across,
+            unit_sems[m][c], chain_sem.at[0], chain_sem.at[1 + 3 * m + c],
+            sums.at[c, :, half[m]], unit_far.at[c, :, half[m]], across,
         )
 
     def begin_unit(c, m):
@@ -646,13 +647,14 @@
                         sums.at[c, pl.ds(first_half, 8), half[m]], work, mat_sem.at[3 * m + c]
                     )
                 )
-        for name, work, come, space, total, pair_sems in (
+        for n, (name, work, come, space, total, pair_sems) in enumerate((
             ("Q", qk_work, qk_came, pair_room, qk_total, (q_send, q_recv)),
             ("V", vg_work, vg_came, pair_room, vg_total, (v_send, v_recv)),
             ("O", out_work, out_came, small_room, out_total, (o_send, o_recv)),
-        ):
+        )):
             chains[name] = Chain(
-                peers, KINDS[name][1], work, come, space, total, pair_sems, chain_sem.at[0]
+                peers, KINDS[name][1], work, come, space, total, pair_sems, chain_sem.at[0],
+                chain_sem.at[7 + n],
             )
         for one in work_loads:
             one.start()
@@ -995,7 +997,7 @@
         dma(4 + 2 * slots),
         dma(9),
         dma(6),
-        dma(1),
+        dma(10),
         *[dma(3 * slots)] * 4,
         *[dma(slots)] * 4,
         *[dma(12)] * 2,

time: 337 us -> 339 us (level)
  no operation moved by 1% of the time
where the time goes in v5:
time: 339 us; the launch traced here: 335 us
  Pallas kernels  331 us (98%)
    pallas_call x1, Pallas kernels, block(): pl.pallas_call(functools.partial(block_kernel, batch), in_specs=[pl.Block...  319 us
    pallas_call x1, Pallas kernels, widen(): pl.pallas_call(widen_kernel, grid=(8,), in_specs=[pl.BlockSpec((3, 8, hid...  11.9 us

profile of v5, /device:TPU:0, one launch (start us, length us, event | category | flops | bytes accessed | tf_op | source)
XLA Modules:
  0.0 334.6 jit_solution(4758373536554167216)
XLA Ops:
  0.6 1.4 select_reduce_fusion.length_ref
  2.0 319.5 %block.1 = (bf16[3,256,1024]{2,1,0:T(8,128)(2,1)}, f32[3,256,1024]{2,1,0:T(8,128)}, bf16[3,8,704,128]{3,2,1,0:T(8,128)(2,1)}, bf16[8,128,512]{2,1,0:T(8,128)(2,1...) custom-call(s32[3]{0:T(128)} %select_reduce_fusion.length_ref, ...), custom_call_target="tpu_custom_call" | custom-call | flops 75296145408 | bytes 88473600 | tf_op jit(solution)/shard_map/block/pallas_call | solution.py:1009
  321.5 0.0 copy-start
  321.5 11.9 %widen.1 = (f32[1024,256]{1,0:T(8,128)}, f32[1024,256]{1,0:T(8,128)}, f32[1024,256]{1,0:T(8,128)}, f32[1024,256]{1,0:T(8,128)}, f32[256,1024]{1,0:T(8,128)}, /*i...) custom-call(bf16[3,8,704,128]{3,2,1,0:T(8,128)(2,1)} %get-tuple-elem, ...), custom_call_target="tpu_custom_call" | custom-call | tf_op jit(solution)/shard_map/widen/pallas_call | solution.py:1051
  333.4 0.0 copy-done
  333.4 0.6 fusion
  334.0 0.6 constant_dynamic-slice_fusion
Async XLA Ops:
  321.5 11.9 %copy-start = (f32[3,1024]{1,0:T(4,128)S(1)}, f32[3,1024]{1,0:T(4,128)}, u32[]{:S(2)}) copy-start(f32[3,1024]{1,0:T(4,128)} %get-tuple-element.46) | copy-start | bytes 36868
